TPU v7x, 512 devices: a whole 4x4x16 slice. The times are simulated.
512 devices in a mesh: row: 32 (over x, z_lo, core), col: 16 (over y, z_hi).
Axes of the slice: x: 4, y: 4, z: 16 (z_hi: 4, z_lo: 4; z = z_hi * 4 + z_lo), core: 2. Of those that a mesh axis runs over, the one named last changes fastest.
Arguments:
- hidden_img: bfloat16 [16384, 2432], P('row', 'col'), may hold values from -75 to 75
- hidden_txt: bfloat16 [3072, 2432], P('row', 'col'), may hold values from -75 to 75
- text_len: int32 [16], replicated, may hold values from 1 to 154, as said below
- step_index: int32 [16], replicated, may hold values from 0 to 27
- latent: float32 [16384, 64], P('row'), may hold values from -6 to 6
- cond: float32 [16, 2432], P(None, 'row'), may hold values from -6 to 6
- mod_weight: bfloat16 [2432, 7, 2432], P('row', None, 'col'), may hold values from -0.125 to 0.125
- qkv_weight: bfloat16 [2432, 3, 2048], P('row', None, 'col'), may hold values from -0.125 to 0.125
- kv_text_weight: bfloat16 [2432, 2, 2048], P('row', None, 'col'), may hold values from -0.125 to 0.125
- q_gain: float32 [64], replicated, may hold values from 0.5 to 6
- k_gain: float32 [2, 64], replicated, may hold values from 0.5 to 6
- out_weight: bfloat16 [2048, 2432], P('row', 'col'), may hold values from -6 to 6
- final_weight: bfloat16 [2432, 64], P('row'), may hold values from -0.125 to 0.125
Outputs:
- velocity: float32 [16384, 64], P('row')
- latent_next: float32 [16384, 64], P('row')
Inputs may be any that keep to these rules, and one draw needn't show every extreme that they name: `text_len`: some request has exactly 154 text tokens in every draw.
All inputs are finite; a program needn't handle non-finite values.
Results may differ from a plain program's by a relative error of at most 0.015.
The roundings to bfloat16 on the way count: a program that leaves them out, or rounds other values in their place, can miss the bound.
Values may be sent and summed in bfloat16 or wider, within the bound.
A program may use at most 64 MiB of HBM per device.

v0:
```python
import jax
import jax.numpy as jnp
from jax import lax
from jax.sharding import PartitionSpec as P

STEPS = 28


EPS_NORM = 1e-06


def partner_2(block, axis, distance):
    count = lax.axis_size(axis)
    route = []
    for low in range(count):
        high = low | 1 << distance
        if high != low and high < count:
            route += [(low, high), (high, low)]
    return lax.ppermute(block, axis, route)


def modulate_full(values, offset, stretch):
    average = jnp.mean(values, axis=1, keepdims=True)
    mean_square = jnp.mean(values * values, axis=1, keepdims=True)
    normed = (values - average) * lax.rsqrt(mean_square - average * average + EPS_NORM)
    return (normed * (1.0 + stretch) + offset).astype(jnp.bfloat16)


def head_norm(values, gain_row):
    mean_square = jnp.mean(values * values, axis=-1, keepdims=True)
    return (values * lax.rsqrt(mean_square + EPS_NORM) * gain_row).astype(jnp.bfloat16)


def sigma_of(step_now):
    remain = 1.0 - step_now.astype(jnp.float32) / STEPS
    return 3.0 * remain / (1.0 + 2.0 * remain)


def per_device(
    hidden_img,
    hidden_txt,
    text_len,
    step_index,
    latent,
    cond,
    mod_weight,
    qkv_weight,
    kv_text_weight,
    q_gain,
    k_gain,
    out_weight,
    final_weight,
):
    row_pos = lax.axis_index("row")
    request = row_pos // 2
    lower_half = row_pos % 2 == 0
    img_rows, width_part = hidden_img.shape
    txt_rows = hidden_txt.shape[0]
    head_dim = q_gain.shape[0]
    qkv_cols = qkv_weight.shape[2]
    heads_here = qkv_cols // head_dim
    activated = jax.nn.silu(cond).astype(jnp.bfloat16)
    mod_local = mod_weight.reshape(mod_weight.shape[0], 7 * width_part)
    mod_terms = jnp.dot(activated, mod_local, preferred_element_type=jnp.float32).reshape(
        activated.shape[0], 7, width_part
    )
    mod_all = lax.psum(mod_terms, "row")
    mod_own = lax.dynamic_index_in_dim(mod_all, request, 0, keepdims=False)
    mod_full = lax.all_gather(mod_own, "col", axis=1, tiled=True)
    img_full, txt_full = (
        lax.all_gather(hidden_img, "col", axis=1, tiled=True),
        lax.all_gather(hidden_txt, "col", axis=1, tiled=True),
    )
    img_ready = modulate_full(img_full.astype(jnp.float32), mod_full[0], mod_full[1])
    txt_ready = modulate_full(txt_full.astype(jnp.float32), mod_full[3], mod_full[4])
    qkv_flat = qkv_weight.reshape(qkv_weight.shape[0], 3 * qkv_cols)
    kv_flat = kv_text_weight.reshape(kv_text_weight.shape[0], 2 * qkv_cols)
    img_proj = jnp.dot(
        img_ready,
        lax.all_gather(qkv_flat, "row", axis=0, tiled=True),
        preferred_element_type=jnp.float32,
    )
    txt_proj = jnp.dot(
        txt_ready,
        lax.all_gather(kv_flat, "row", axis=0, tiled=True),
        preferred_element_type=jnp.float32,
    )
    img_proj = img_proj.reshape(img_rows, 3, heads_here, head_dim)
    txt_proj = txt_proj.reshape(txt_rows, 2, heads_here, head_dim)
    queries = head_norm(img_proj[:, 0], q_gain)
    img_keys = head_norm(img_proj[:, 1], k_gain[0])
    img_values = img_proj[:, 2].astype(jnp.bfloat16)
    txt_keys = head_norm(txt_proj[:, 0], k_gain[1])
    txt_values = txt_proj[:, 1].astype(jnp.bfloat16)
    length = lax.dynamic_index_in_dim(text_len, request, 0, keepdims=False)
    scaling = head_dim ** (-0.5)
    partner = partner_2((img_keys, img_values, txt_keys, txt_values), "row", 0)

    def ordered(own_part, peer_part):
        return jnp.concatenate(
            [
                jnp.where(lower_half, own_part, peer_part),
                jnp.where(lower_half, peer_part, own_part),
            ],
            axis=0,
        )

    all_keys = jnp.concatenate(
        [ordered(img_keys, partner[0]), ordered(txt_keys, partner[2])], axis=0
    )
    all_values = jnp.concatenate(
        [ordered(img_values, partner[1]), ordered(txt_values, partner[3])], axis=0
    )
    key_valid = jnp.concatenate(
        [jnp.ones((2 * img_rows,), dtype=bool), jnp.arange(2 * txt_rows) < length]
    )

    def attend(head_ops):
        q_head, k_head, v_head = head_ops
        scores = jnp.dot(q_head, k_head.T, preferred_element_type=jnp.float32) * scaling
        scores = jnp.where(key_valid[None, :], scores, -jnp.inf)
        row_max = jnp.max(scores, axis=1, keepdims=True)
        weights = jnp.exp(scores - row_max)
        probabilities = (weights / jnp.sum(weights, axis=1, keepdims=True)).astype(jnp.bfloat16)
        return jnp.dot(probabilities, v_head, preferred_element_type=jnp.float32).astype(
            jnp.bfloat16
        )

    attended = lax.map(
        attend,
        (jnp.moveaxis(queries, 1, 0), jnp.moveaxis(all_keys, 1, 0), jnp.moveaxis(all_values, 1, 0)),
    )
    attended = jnp.moveaxis(attended, 0, 1).reshape(img_rows, qkv_cols)
    full_heads = lax.all_gather(attended, "col", axis=1, tiled=True)
    projected = jnp.dot(
        full_heads,
        lax.all_gather(out_weight, "row", axis=0, tiled=True),
        preferred_element_type=jnp.float32,
    )
    updated = (hidden_img.astype(jnp.float32) + mod_own[2] * projected).astype(jnp.bfloat16)
    head_full = lax.all_gather(final_weight, "row", axis=0, tiled=True)
    residual = lax.all_gather(updated, "col", axis=1, tiled=True)
    head_in = modulate_full(residual.astype(jnp.float32), mod_full[5], mod_full[6])
    velocity = jnp.dot(head_in, head_full, preferred_element_type=jnp.float32)
    step_now = lax.dynamic_index_in_dim(step_index, request, 0, keepdims=False)
    sigma_step = sigma_of(step_now + 1) - sigma_of(step_now)
    latent_next = latent + sigma_step * velocity
    return (velocity, latent_next)


def solution(mesh):
    in_specs = (
        P("row", "col"),
        P("row", "col"),
        P(),
        P(),
        P("row", None),
        P(None, "row"),
        P("row", None, "col"),
        P("row", None, "col"),
        P("row", None, "col"),
        P(),
        P(),
        P("row", "col"),
        P("row", None),
    )
    out_specs = (P("row", None), P("row", None))
    return jax.shard_map(
        per_device, mesh=mesh, in_specs=in_specs, out_specs=out_specs, check_vma=False
    )
```

profile of v0, /device:TPU:6, one launch (start us, length us, event | category | flops | bytes accessed | tf_op | source)
XLA Modules:
  0.0 752.9 jit_solution(9680876865259763626)
XLA Ops:
  7.2 0.9 copy-done
  8.1 1.6 fusion.48
  9.8 1.4 reshape.166
  11.3 0.9 copy.53
  13.6 1.2 dynamic_slice.23
  15.4 66.6 %all_gather.30 = bf16[96,2432]{0,1:T(8,128)(2,1)S(1)} all-gather(bf16[96,152]{0,1:T(8,128)(2,1)} %param.16), channel_id=1, replica_groups=mesh['row'=32,'col'=16] {'col'}, dimensions={1}, use_global_device_ids=true | all-gather | bytes 496128 | tf_op jit(solution)/shard_map/all_gather | solution.py:72
  82.3 1.3 slice_bitcast_fusion.3
  83.6 178.8 %all-reduce.3.cloned.1.call-done = f32[16,7,152]{2,0,1:T(8,128)} async-done(((f32[16,7,152]{2,0,1:T(8,128)}), f32[16,7,152]{2,0,1:T(8,128)}) %all-reduce.3.cloned.1.call-update) | async-done | bytes 68112 | tf_op jit(solution)/shard_map/psum | solution.py:67
  262.4 0.8 constant_dynamic-slice_fusion.1
  263.3 77.2 %all-gather = f32[1,7,2432]{1,0,2:T(1,128)S(1)} all-gather(f32[1,7,152]{1,0,2:T(1,128)S(1)} %copy.52), channel_id=2, replica_groups=mesh['row'=32,'col'=16] {'col'}, dimensions={2}, use_global_device_ids=true | all-gather | bytes 72352 | tf_op jit(solution)/shard_map/all_gather | solution.py:69
  340.6 42.9 %fusion.39 = (f32[2432]{0:T(1024)}, f32[2432]{0:T(1024)S(1)}, f32[2432]{0:T(1024)S(1)}, f32[2432]{0:T(1024)}, f32[2432]{0:T(1024)}, /*index=5*/f32[2432]{0:T(1024)}) fusion(f32[1,7,2432]{1,0,2:T(1,128)S(1)} %all-gather), kind=kLoop, calls=%fused_computation.55 | loop fusion | flops 7296 | bytes 116736 | tf_op jit(solution)/shard_map/add | solution.py:26
  383.4 2.2 reshape.167
  385.6 1.3 fusion.42
  386.9 2.0 collective-permute-start.3
  389.0 2.3 collective-permute-start.1
  392.9 32.3 %all-gather.16.cloned.1.call-done = bf16[32,76,384]{2,1,0:T(8,128)(2,1)} async-done(((bf16[1,76,384]{2,1,0:T(8,128)(2,1)}), bf16[32,76,384]{2,1,0:T(8,128)(2,1)}) %all-gather.16.cloned.1.call-update) | async-done | bytes 1867792 | tf_op jit(solution)/shard_map/all_gather | solution.py:80
  425.3 2.5 reshape.165
  427.7 105.3 %all-gather.10.cloned.1.call-done = bf16[512,2432]{0,1:T(8,128)(2,1)} async-done(((bf16[512,152]{0,1:T(8,128)(2,1)}), bf16[512,2432]{0,1:T(8,128)(2,1)}) %all-gather.10.cloned.1.call-update) | async-done | bytes 2490384 | tf_op jit(solution)/shard_map/all_gather | solution.py:71
  533.0 2.6 convert_reduce_fusion.1
  535.6 1.9 fusion.24
  537.7 1.9 collective-permute-start
  539.7 2.6 collective-permute-start.2
  542.3 0.9 concatenate.10
  543.4 3.1 while.10
  547.3 42.3 %all_gather.33 = bf16[2048,152]{1,0:T(8,128)(2,1)S(1)} all-gather(bf16[64,152]{1,0:T(8,128)(2,1)S(1)} %copy-done.6), channel_id=1, replica_groups=mesh['row'=32,'col'=16] {'row'}, dimensions={0}, use_global_device_ids=true | all-gather | bytes 642048 | tf_op jit(solution)/shard_map/all_gather | solution.py:137
  590.2 47.3 %all-gather.12.cloned.1.call-done = bf16[512,2048]{0,1:T(8,128)(2,1)} async-done(((bf16[512,128]{0,1:T(8,128)(2,1)}), bf16[512,2048]{0,1:T(8,128)(2,1)}) %all-gather.12.cloned.1.call-update) | async-done | bytes 2097168 | tf_op jit(solution)/shard_map/all_gather | solution.py:134
  637.6 2.8 fusion.41
  642.4 41.5 %all-gather.3 = bf16[32,76,64]{1,2,0:T(8,128)(2,1)S(1)} all-gather(bf16[1,76,64]{1,2,0:T(8,128)(2,1)S(1)} %bitcast.104), channel_id=1, replica_groups=mesh['row'=32,'col'=16] {'row'}, dimensions={0}, use_global_device_ids=true | all-gather | bytes 321024 | tf_op jit(solution)/shard_map/all_gather | solution.py:141
  684.2 0.8 reshape.169
  685.0 56.6 %all-gather.14.cloned.1.call-done = bf16[512,2432]{0,1:T(8,128)(2,1)} async-done(((bf16[512,152]{0,1:T(8,128)(2,1)}), bf16[512,2432]{0,1:T(8,128)(2,1)}) %all-gather.14.cloned.1.call-update) | async-done | bytes 2490384 | tf_op jit(solution)/shard_map/all_gather | solution.py:142
  741.7 2.6 convert_reduce_fusion
  744.3 1.8 multiply_add_fusion
  (79 shorter events, 10.0 us)
Async XLA Ops:
  7.2 1.0 copy-start
  7.2 255.2 %all-reduce.3.cloned.1.call-start = ((), (), s32[]{:S(2)}) async-start(), calls=%async_computation | async-start | bytes 229376 | tf_op jit(solution)/shard_map/psum | solution.py:67
  9.8 373.7 %all-gather.18.cloned.1.call-start = ((), (), s32[]{:S(2)}) async-start(), calls=%async_computation.5 | async-start | bytes 1351680 | tf_op jit(solution)/shard_map/all_gather | solution.py:85
  11.3 414.0 %all-gather.16.cloned.1.call-start = ((), (), s32[]{:S(2)}) async-start(), calls=%async_computation.4 | async-start | bytes 2027520 | tf_op jit(solution)/shard_map/all_gather | solution.py:80
  12.9 520.1 %all-gather.10.cloned.1.call-start = ((), (), s32[]{:S(2)}) async-start(), calls=%async_computation.1 | async-start | bytes 2646016 | tf_op jit(solution)/shard_map/all_gather | solution.py:71
  13.5 624.1 %all-gather.12.cloned.1.call-start = ((), (), s32[]{:S(2)}) async-start(), calls=%async_computation.2 | async-start | bytes 2228224 | tf_op jit(solution)/shard_map/all_gather | solution.py:134
  386.9 4.5 collective-permute-start.3
  389.0 3.2 collective-permute-start.1
  392.9 142.7 %copy-start.10 = (f32[2432]{0:T(1024)S(1)}, f32[2432]{0:T(1024)}, u32[]{:S(2)}) copy-start(f32[2432]{0:T(1024)} %get-tuple-element.48) | copy-start | bytes 29188
  392.9 142.7 %copy-start.11 = (f32[2432]{0:T(1024)S(1)}, f32[2432]{0:T(1024)}, u32[]{:S(2)}) copy-start(f32[2432]{0:T(1024)} %get-tuple-element.49) | copy-start | bytes 29188
  533.0 2.6 copy-start.1
  535.6 2.0 copy-start.12
  535.6 2.0 copy-start.13
  537.5 5.8 copy-start.5
  537.7 4.6 collective-permute-start
  539.7 3.6 collective-permute-start.2
  543.4 3.8 copy-start.6
  543.4 94.2 %copy-start.3 = (bf16[512,152]{0,1:T(8,128)(2,1)S(1)}, bf16[512,152]{0,1:T(8,128)(2,1)}, u32[]{:S(2)}) copy-start(bf16[512,152]{0,1:T(8,128)(2,1)} %param.15) | copy-start | bytes 466948
  546.5 0.7 copy-start.4
  546.5 93.9 %copy-start.15 = (s32[16]{0:T(128)S(1)}, s32[16]{0:T(128)}, u32[]{:S(2)}) copy-start(s32[16]{0:T(128)} %param.18) | copy-start | bytes 196
  546.5 95.8 %copy-start.7 = (bf16[76,64]{0,1:T(8,128)(2,1)S(1)}, bf16[76,64]{0,1:T(8,128)(2,1)}, u32[]{:S(2)}) copy-start(bf16[76,64]{0,1:T(8,128)(2,1)} %param.27) | copy-start | bytes 29188
  547.2 194.5 %all-gather.14.cloned.1.call-start = ((), (), s32[]{:S(2)}) async-start(), calls=%async_computation.3 | async-start | bytes 2646016 | tf_op jit(solution)/shard_map/all_gather | solution.py:142
  640.4 103.8 %copy-start.8 = (f32[2432]{0:T(1024)S(1)}, f32[2432]{0:T(1024)}, u32[]{:S(2)}) copy-start(f32[2432]{0:T(1024)} %get-tuple-element.45) | copy-start | bytes 29188
  640.4 103.8 %copy-start.9 = (f32[2432]{0:T(1024)S(1)}, f32[2432]{0:T(1024)}, u32[]{:S(2)}) copy-start(f32[2432]{0:T(1024)} %get-tuple-element.50) | copy-start | bytes 29188
  640.5 103.8 %copy-start.14 = (f32[512,64]{0,1:T(8,128)S(1)}, f32[512,64]{0,1:T(8,128)}, u32[]{:S(2)}) copy-start(f32[512,64]{0,1:T(8,128)} %param.19) | copy-start | bytes 393220
  741.7 2.6 copy-start.2
Sparse Core Ops, SparseCore 0:
  11.5 250.8 all-reduce.2
  264.8 91.0 all-gather.17
  358.8 66.3 all-gather.15
  428.6 104.3 all-gather.9
  547.3 90.2 all-gather.11
  640.9 100.6 all-gather.13
where the time goes:
time: 754 us; the launch traced here: 753 us
  waiting for transfers between devices  421 us (56%)
  blocking collectives  228 us (30%)
  other arithmetic  51.4 us (7%)
  local copies, waits for them, and re-layouts  16 us (2%)
  between operations  15.9 us (2%)
  matrix products  11.6 us (2%)
  starting transfers between devices  9.08 us (1%)
    psum x1, waiting for transfers between devices, per_device(): mod_all = lax.psum(mod_terms, 'row')  179 us
    all_gather x1, waiting for transfers between devices, per_device(): lax.all_gather(hidden_img, 'col', axis=1, tiled=True)  105 us
    all_gather x1, blocking collectives, per_device(): mod_full = lax.all_gather(mod_own, 'col', axis=1, tiled=True)  77.2 us
    all_gather x1, blocking collectives, per_device(): lax.all_gather(hidden_txt, 'col', axis=1, tiled=True)  66.6 us
    all_gather x1, waiting for transfers between devices, per_device(): residual = lax.all_gather(updated, 'col', axis=1, tiled=True)  56.6 us
    all_gather x1, waiting for transfers between devices, per_device(): full_heads = lax.all_gather(attended, 'col', axis=1, tiled=True)  47.3 us
    add x1, other arithmetic, modulate_full(): return (normed * (1.0 + stretch) + offset).astype(jnp.bfloat16)  42.9 us
    all_gather x1, blocking collectives, per_device(): lax.all_gather(out_weight, 'row', axis=0, tiled=True)  42.3 us
  transfers between devices with their start and end apart: 10, of which 6 were waited for; matrix products, arithmetic and copies ran while one was open for 8% of the time, Pallas kernels for 0%

commit v1 on v0

v1 whole, which is shorter than its diff:
```python
import jax
import jax.numpy as jnp
from jax import lax
from jax.experimental import pallas as pl
from jax.experimental.pallas import tpu as pltpu
from jax.sharding import PartitionSpec as P

STEPS = 28
EPS_NORM = 1e-06
WIDTH = 2432
MESH = pl.DeviceIdType.MESH
BF = jnp.bfloat16
F32 = jnp.float32
ANY = pl.BlockSpec(memory_space=pl.ANY)
VMEM = pl.BlockSpec(memory_space=pltpu.VMEM)
SMEM = pl.BlockSpec(memory_space=pltpu.SMEM)


def place():
    r, c = lax.axis_index("row"), lax.axis_index("col")
    return r // 8, (r // 2) % 4, r % 2, c // 4, c % 4


def device(x, zl, core, y, zh):
    return ((x * 4 + zl) * 2 + core, y * 4 + zh)


def up(v, d, n=4):
    return lax.rem(v + d + n, n)


def meet(devices):
    barrier = pltpu.get_barrier_semaphore()
    for d in devices:
        pl.semaphore_signal(barrier, inc=1, device_id=d, device_id_type=MESH)
    pl.semaphore_wait(barrier, len(devices))


class Post:
    def __init__(self, send_sem, recv_sem):
        self.send_sem, self.recv_sem, self.n, self.sent = send_sem, recv_sem, 0, []

    def send(self, src, dst, to, got):
        k = self.n
        self.n += 1
        copy = pltpu.make_async_remote_copy(
            src_ref=src, dst_ref=dst, send_sem=self.send_sem.at[k], recv_sem=self.recv_sem.at[k],
            device_id=to, device_id_type=MESH)
        copy.start()
        self.sent.append(copy)
        back = pltpu.make_async_remote_copy(
            src_ref=got, dst_ref=got, send_sem=self.send_sem.at[k], recv_sem=self.recv_sem.at[k],
            device_id=to, device_id_type=MESH)
        return back.wait_recv

    def finish(self):
        for copy in self.sent:
            copy.wait_send()


def gather_kernel(x_in, w_in, ow_in, mp, X, W, OW, M, part, tot, send_sem, recv_sem, own_sem):
    x, zl, core, y, zh = place()
    me = x * 4 + zl
    zg = zh * 4 + zl

    def at_chip(q):
        return (q * 2 + core, y * 4 + zh)

    def at_x(d):
        return device(up(x, d), zl, core, y, zh)

    def at_y(d):
        return device(x, zl, core, up(y, d), zh)

    def at_zh(d):
        return device(x, zl, core, y, up(zh, d))

    def at_zl(d):
        return device(x, up(zl, d), core, y, zh)

    def at_z(d):
        z = up(zg, d, 16)
        return device(x, lax.rem(z, 4), core, y, z // 4)

    partner = device(x, zl, 1 - core, y, zh)
    meet([at_chip(up(me, d, 16)) for d in range(1, 16)] + [at_zh(d) for d in (1, 2, 3)]
         + [at_y(d) for d in (1, 2, 3)] + [at_z(1), at_z(-1), partner])
    post = Post(send_sem, recv_sem)
    local = [pltpu.make_async_copy(x_in, X.at[y, zh], own_sem.at[0]),
             pltpu.make_async_copy(w_in, W.at[core, x, zl], own_sem.at[1]),
             pltpu.make_async_copy(ow_in, OW.at[core, x, zg], own_sem.at[2])]

    mods = []
    for d in range(1, 16):
        q, p = up(me, d, 16), up(me, -d, 16)
        mods.append(post.send(mp.at[q], part.at[me], at_chip(q), part.at[p]))
    zp = post.send(x_in, X.at[y, zh], at_zh(1), X.at[y, up(zh, -1)])
    zm = post.send(x_in, X.at[y, zh], at_zh(-1), X.at[y, up(zh, 1)])
    low, high = pl.ds(0, 80), pl.ds(80, 80)

    def y_out(z, src=None):
        s = X.at[y, z] if src is None else src
        return (post.send(s, X.at[y, z], at_y(1), X.at[up(y, -1), z]),
                post.send(s, X.at[y, z], at_y(-1), X.at[up(y, 1), z]))

    def y_on(z, waits):
        waits[0]()
        a = X.at[up(y, -1), z, low]
        f = post.send(a, a, at_y(1), X.at[up(y, 2), z, low])
        waits[1]()
        b = X.at[up(y, 1), z, high]
        g = post.send(b, b, at_y(-1), X.at[up(y, 2), z, high])
        return f, g

    y0 = y_out(zh, x_in)
    w_z = [post.send(w_in, W.at[core, x, zl], at_zl(d), W.at[core, x, up(zl, -d)]) for d in (1, 2, 3)]

    def ring(s):
        if s < 8:
            a, b = up(zg, 1 - s, 16), up(zg, s - 1, 16)
            p = ow_in if s == 1 else OW.at[core, x, a]
            q = ow_in if s == 1 else OW.at[core, x, b]
            return (post.send(p, OW.at[core, x, a], at_z(1), OW.at[core, x, up(zg, -s, 16)]),
                    post.send(q, OW.at[core, x, b], at_z(-1), OW.at[core, x, up(zg, s, 16)]))
        t, u = pl.ds(0, 32), pl.ds(32, 32)
        a, b = OW.at[core, x, up(zg, -7, 16), t], OW.at[core, x, up(zg, 7, 16), u]
        return (post.send(a, a, at_z(1), OW.at[core, x, up(zg, 8, 16), t]),
                post.send(b, b, at_z(-1), OW.at[core, x, up(zg, 8, 16), u]))

    def ring_on(s, waits):
        waits[0]()
        waits[1]()
        return ring(s + 1) if s < 8 else None

    step = ring(1)
    for copy in local:
        copy.start()

    for wait in mods:
        wait()
    part[me] = mp[me]
    total = part[0]
    for i in range(1, 16):
        total = total + part[i]
    tot[core] = total
    tw = post.send(tot.at[core], tot.at[core], partner, tot.at[1 - core])
    step = ring_on(1, step)
    y0f = y_on(zh, y0)
    tw()
    M[y, zh] = tot[0] + tot[1]
    m_z = [post.send(M.at[y, zh], M.at[y, zh], at_zh(d), M.at[y, up(zh, -d)]) for d in (1, 2, 3)]
    local[1].wait()
    for wait in w_z:
        wait()

    def x_out(ref):
        s = ref.at[core, x]
        return (post.send(s, s, at_x(1), ref.at[core, up(x, -1)]),
                post.send(s, s, at_x(-1), ref.at[core, up(x, 1)]))

    def x_on(ref, waits, half):
        waits[0]()
        a = ref.at[core, up(x, -1), pl.ds(0, half)]
        f = post.send(a, a, at_x(1), ref.at[core, up(x, 2), pl.ds(0, half)])
        waits[1]()
        b = ref.at[core, up(x, 1), pl.ds(half, half)]
        g = post.send(b, b, at_x(-1), ref.at[core, up(x, 2), pl.ds(half, half)])
        return f, g

    def across(ref, d):
        s = ref.at[core, up(x, d)]
        return post.send(s, s, partner, ref.at[1 - core, up(x, d)])

    last = []
    w_x = x_out(W)
    last.append(across(W, 0))
    step = ring_on(2, step)
    for wait in m_z:
        wait()
    last += [post.send(M.at[y], M.at[y], at_y(d), M.at[up(y, -d)]) for d in (1, 2, 3)]
    zp()
    a = X.at[y, up(zh, -1), low]
    zpf = post.send(a, a, at_zh(1), X.at[y, up(zh, 2), low])
    y1 = y_out(up(zh, -1))
    zm()
    b = X.at[y, up(zh, 1), high]
    zmf = post.send(b, b, at_zh(-1), X.at[y, up(zh, 2), high])
    y2 = y_out(up(zh, 1))
    step = ring_on(3, step)
    w_xf = x_on(W, w_x, 2)
    last += [across(W, -1), across(W, 1)]
    step = ring_on(4, step)
    y1f = y_on(up(zh, -1), y1)
    y2f = y_on(up(zh, 1), y2)
    step = ring_on(5, step)
    zpf()
    zmf()
    y3 = y_out(up(zh, 2))
    step = ring_on(6, step)
    step = ring_on(7, step)
    w_xf[0]()
    w_xf[1]()
    last.append(across(W, 2))
    ring_on(8, step)
    local[2].wait()
    o_x = x_out(OW)
    last.append(across(OW, 0))
    y3f = y_on(up(zh, 2), y3)
    for waits in (y0f, y1f, y2f, y3f):
        waits[0]()
        waits[1]()
    o_xf = x_on(OW, o_x, 8)
    last += [across(OW, -1), across(OW, 1)]
    o_xf[0]()
    o_xf[1]()
    last.append(across(OW, 2))
    for wait in last:
        wait()
    local[0].wait()
    post.finish()


def tdot(a, b):
    return lax.dot_general(a, b, (((0,), (0,)), ((), ())), preferred_element_type=F32)


def attention_kernel(X, W, M, G, text_len, out, ready, KB, VB, send_sem, recv_sem):
    x, zl, core, y, zh = place()
    partner = device(x, zl, 1 - core, y, zh)
    meet([partner])
    post = Post(send_sem, recv_sem)

    def tally(c, carry):
        v = X[c].astype(F32)
        s, q = carry
        return s + v.reshape(20, 8, 640).sum(axis=0), q + (v * v).reshape(20, 8, 640).sum(axis=0)

    zero = jnp.zeros((8, 640), F32)
    s, q = lax.fori_loop(0, 16, tally, (zero, zero))
    mean = jnp.sum(s, axis=0, keepdims=True) / WIDTH
    square = jnp.sum(q, axis=0, keepdims=True) / WIDTH
    rs = lax.rsqrt(square - mean * mean + EPS_NORM)

    def make_ready(c, carry):
        v = (X[c].astype(F32) - mean) * rs
        m = M[c].T
        a = v[:, :512] * (1.0 + m[:160, 1:2]) + m[:160, 0:1]
        b = v[:, 512:] * (1.0 + m[:160, 4:5]) + m[:160, 3:4]
        r = jnp.concatenate([a, b], axis=1).astype(BF)
        ready[pl.ds(pl.multiple_of(80 * c, 16), 80)] = r[:80]
        ready[pl.ds(pl.multiple_of(1280 + 80 * c, 16), 80)] = r[80:]
        return carry

    lax.fori_loop(0, 16, make_ready, 0)

    def normed(u, g):
        square = jnp.mean(u * u, axis=0, keepdims=True)
        return u * lax.rsqrt(square + EPS_NORM) * g

    def two(u, g):
        return jnp.concatenate([normed(u[:64], g), normed(u[64:], g)], axis=0)

    kv = tdot(W[:, 128:384], ready[:, :512])
    tkv = tdot(W[:, 384:640], ready[:, 512:])
    KB[0, :512] = two(kv[:128], G[:, 1:2]).T.astype(BF)
    KB[0, 512:] = two(tkv[:128], G[:, 2:3]).T.astype(BF)
    VB[0, :, :512] = kv[128:].astype(BF)
    VB[0, :, 512:] = tkv[128:].astype(BF)
    waits = [post.send(KB.at[0], KB.at[1], partner, KB.at[1]),
             post.send(VB.at[0], VB.at[1], partner, VB.at[1])]
    qt = two(tdot(W[:, :128], ready[:, :512]), G[:, 0:1])
    head = lax.broadcasted_iota(jnp.int32, (128, 512), 0) // 64
    qz = [jnp.where(head == h, qt, 0.0).astype(BF) for h in range(2)]
    for wait in waits:
        wait()
    length = text_len[x * 4 + zl]
    slot = lax.broadcasted_iota(jnp.int32, (128, 256), 0)
    valid = [(slot < 96) & (slot + 96 * owner < length) for owner in (core, 1 - core)]
    for part in range(2):
        for h in range(2):
            t = qz[h][:, 256 * part:256 * part + 256]
            scores = []
            for j in range(2):
                sc = jnp.dot(KB[j], t, preferred_element_type=F32) * 0.125
                scores += [sc[:512], jnp.where(valid[j], sc[512:], -jnp.inf)]
            top = scores[0].max(axis=0, keepdims=True)
            for sc in scores[1:]:
                top = jnp.maximum(top, sc.max(axis=0, keepdims=True))
            e = [jnp.exp(sc - top) for sc in scores]
            total = sum(v.sum(axis=0, keepdims=True) for v in e)
            inv = 1.0 / total
            p = [(v * inv).astype(BF) for v in e]
            o = 0.0
            for j in range(2):
                o = o + jnp.dot(VB[j, 64 * h:64 * h + 64, :512], p[2 * j], preferred_element_type=F32)
                o = o + jnp.dot(VB[j, 64 * h:64 * h + 64, 512:], p[2 * j + 1], preferred_element_type=F32)
            out[h, :, 256 * part:256 * part + 256] = o.astype(BF)
    post.finish()


def tail_kernel(att, X, M, OW, out, A, H, acc, U, ST, VP, VZ, send_sem, recv_sem, own_sem):
    x, zl, core, y, zh = place()

    def at_y(d):
        return device(x, zl, core, up(y, d), zh)

    def at_zh(d):
        return device(x, zl, core, y, up(zh, d))

    meet([at_y(d) for d in (1, 2, 3)] + [at_zh(d) for d in (1, 2, 3)])
    post = Post(send_sem, recv_sem)

    def lanes(z):
        return pl.ds(pl.multiple_of(128 * z, 128), 128)

    waits = []
    for d in (1, 3, 2):
        t = up(zh, d)
        waits.append(post.send(att.at[:, :, lanes(t)], A.at[:, y, zh], at_zh(d), A.at[:, y, up(zh, -d)]))
    local = [pltpu.make_async_copy(att.at[:, :, lanes(zh)], A.at[:, y, zh], own_sem.at[0]),
             pltpu.make_async_copy(X.at[y, :, :, lanes(zh)], H, own_sem.at[1])]
    for copy in local:
        copy.start()
    local[0].wait()
    for wait in waits:
        wait()
    ys = [post.send(A.at[:, y], A.at[:, y], at_y(d), A.at[:, up(y, -d)]) for d in (1, 3, 2)]

    def project(yy, first):
        for z in range(4):
            t = 0.0
            for h in range(2):
                a = A[h, yy].reshape(256, 128)
                w = OW[h, yy, 4 * z:4 * z + 4].reshape(256, 256)
                t = t + tdot(a, w)
            acc[z] = t if first else acc[z] + t

    project(y, True)
    for wait, d in zip(ys, (1, 3, 2)):
        wait()
        project(up(y, -d), False)
    local[1].wait()
    s = q = jnp.zeros((8, 128), F32)
    for z in range(4):
        m = M[4 * y + z].T
        u = (H[z].astype(F32) + m[:160, 2:3] * acc[z].T[:160]).astype(BF)
        U[z] = u
        v = u.astype(F32).reshape(20, 8, 128)
        s = s + v.sum(axis=0)
        q = q + (v * v).sum(axis=0)
    ST[y, 0] = s
    ST[y, 1] = q
    waits = [post.send(ST.at[y], ST.at[y], at_y(d), ST.at[up(y, -d)]) for d in (1, 3, 2)]
    for wait in waits:
        wait()
    st = ST[0] + ST[1] + (ST[2] + ST[3])
    mean = jnp.sum(st[0], axis=0, keepdims=True) / WIDTH
    square = jnp.sum(st[1], axis=0, keepdims=True) / WIDTH
    rs = lax.rsqrt(square - mean * mean + EPS_NORM)
    vel = 0.0
    for z in range(4):
        m = M[4 * y + z].T
        hi = (((U[z].astype(F32) - mean) * rs) * (1.0 + m[:160, 6:7]) + m[:160, 5:6]).astype(BF)
        for h in range(2):
            f = OW[h, y, z][:, 160:240]
            vel = vel + jnp.dot(f, hi[80 * h:80 * h + 80], preferred_element_type=F32)
    VP[y] = vel
    waits = [post.send(VP.at[y], VP.at[y], at_y(d), VP.at[up(y, -d)]) for d in (1, 3, 2)]
    for wait in waits:
        wait()
    VZ[zh] = VP[0] + VP[1] + (VP[2] + VP[3])
    waits = [post.send(VZ.at[zh], VZ.at[zh], at_zh(d), VZ.at[up(zh, -d)]) for d in (1, 3, 2)]
    for wait in waits:
        wait()
    for z in range(4):
        out[:, 128 * z:128 * z + 128] = VZ[z]
    post.finish()


def params(n, mb=60):
    return pltpu.CompilerParams(collective_id=n, has_side_effects=True, vmem_limit_bytes=mb << 20)


def sigma_of(step_now):
    remain = 1.0 - step_now.astype(F32) / STEPS
    return 3.0 * remain / (1.0 + 2.0 * remain)


def dma(n):
    return pltpu.SemaphoreType.DMA((n,))


def split80(v, axis):
    shape = v.shape
    v = v.reshape(shape[:axis] + (2, 76) + shape[axis + 1:])
    pads = [(0, 0)] * v.ndim
    pads[axis + 1] = (0, 4)
    return jnp.pad(v, pads).reshape(shape[:axis] + (160,) + shape[axis + 1:])


def per_device(hidden_img, hidden_txt, text_len, step_index, latent, cond, mod_weight, qkv_weight,
               kv_text_weight, q_gain, k_gain, out_weight, final_weight):
    activated = jax.nn.silu(cond).astype(BF)
    terms = jnp.dot(activated, mod_weight.reshape(76, 7 * 152), preferred_element_type=F32)
    terms = jnp.pad(split80(terms.reshape(16, 7, 152), 2), ((0, 0), (0, 1), (0, 96)))
    both = jnp.concatenate([hidden_img, hidden_txt, jnp.zeros((32, 152), BF)], axis=0)
    x_in = split80(both.T, 0)
    w_in = jnp.concatenate([qkv_weight.reshape(76, 384), kv_text_weight.reshape(76, 256)], axis=1)
    w_in = jnp.pad(w_in, ((0, 4), (0, 0)))
    ow_in = jnp.concatenate([split80(out_weight, 1), jnp.pad(final_weight.T, ((0, 0), (0, 20)))], axis=1)
    gains = jnp.pad(jnp.stack([q_gain, k_gain[0], k_gain[1]], axis=1), ((0, 0), (0, 125)))
    X, W, OW, M = pl.pallas_call(
        gather_kernel,
        out_shape=(jax.ShapeDtypeStruct((4, 4, 160, 640), BF), jax.ShapeDtypeStruct((2, 4, 4, 80, 640), BF),
                   jax.ShapeDtypeStruct((2, 4, 16, 64, 256), BF), jax.ShapeDtypeStruct((4, 4, 8, 256), F32)),
        in_specs=[ANY, ANY, ANY, VMEM],
        out_specs=(ANY, ANY, ANY, VMEM),
        scratch_shapes=[pltpu.VMEM((16, 8, 256), F32), pltpu.VMEM((2, 8, 256), F32), dma(80), dma(80), dma(3)],
        compiler_params=params(0),
        name="gather",
    )(x_in, w_in, ow_in, terms)
    M = M.reshape(16, 8, 256)
    att = pl.pallas_call(
        attention_kernel,
        out_shape=jax.ShapeDtypeStruct((2, 64, 512), BF),
        in_specs=[VMEM, VMEM, VMEM, VMEM, SMEM],
        out_specs=VMEM,
        scratch_shapes=[pltpu.VMEM((2560, 640), BF), pltpu.VMEM((2, 640, 128), BF),
                        pltpu.VMEM((2, 128, 640), BF), dma(2), dma(2)],
        compiler_params=params(1),
        name="attention",
    )(X.reshape(16, 160, 640), W.reshape(2560, 640), M, gains, text_len)
    vel = pl.pallas_call(
        tail_kernel,
        out_shape=jax.ShapeDtypeStruct((64, 512), F32),
        in_specs=[ANY, ANY, VMEM, VMEM],
        out_specs=VMEM,
        scratch_shapes=[pltpu.VMEM((2, 4, 4, 64, 128), BF), pltpu.VMEM((4, 160, 128), BF),
                        pltpu.VMEM((4, 128, 256), F32), pltpu.VMEM((4, 160, 128), BF),
                        pltpu.VMEM((4, 2, 8, 128), F32), pltpu.VMEM((4, 64, 128), F32),
                        pltpu.VMEM((4, 64, 128), F32), dma(16), dma(16), dma(2)],
        compiler_params=params(2),
        name="tail",
    )(att, X, M, OW)
    velocity = vel.T
    step_now = lax.dynamic_index_in_dim(step_index, lax.axis_index("row") // 2, 0, keepdims=False)
    sigma_step = sigma_of(step_now + 1) - sigma_of(step_now)
    return velocity, latent + sigma_step * velocity


def solution(mesh):
    in_specs = (P("row", "col"), P("row", "col"), P(), P(), P("row", None), P(None, "row"),
                P("row", None, "col"), P("row", None, "col"), P("row", None, "col"), P(), P(),
                P("row", "col"), P("row", None))
    out_specs = (P("row", None), P("row", None))
    return jax.shard_map(per_device, mesh=mesh, in_specs=in_specs, out_specs=out_specs, check_vma=False)
```

time: 754 us -> 183 us (0.24)
  waiting for transfers between devices: 421 us -> 0 us
  blocking collectives: 228 us -> 0 us
  Pallas kernels: 0 us -> 165 us
  other arithmetic: 51.4 us -> 4.64 us
  between operations: 15.9 us -> 2.22 us
  matrix products: 11.6 us -> 0.86 us
  starting transfers between devices: 9.08 us -> 0 us
    all_gather x5 -> x0, waiting for transfers between devices: 242 us -> none  [the longest x1 105 us: per_device(): lax.all_gather(hidden_img, 'col', axis=1, tiled=True)]
    all_gather x4 -> x0, blocking collectives: 228 us -> none  [the longest x1 77.2 us: per_device(): mod_full = lax.all_gather(mod_own, 'col', axis=1, tiled=True)]
    psum x1 -> x0, waiting for transfers between devices: 179 us -> none  [per_device(): mod_all = lax.psum(mod_terms, 'row')]
    pallas_call x0 -> x3, Pallas kernels: none -> 165 us  [the longest x1 102 us: per_device(): pl.pallas_call(gather_kernel, out_shape=(jax.ShapeDtypeStruct((4, 4, 160,...]
    add x1, other arithmetic: 42.9 us -> 1.58 us  [per_device(): return (velocity, latent + sigma_step * velocity)]
    dot_general x9 -> x1, matrix products: 11.6 us -> 0.86 us  [per_device(): jnp.dot(activated, mod_weight.reshape(76, 7 * 152), preferred_element_typ...]
    ppermute x4 -> x0, starting transfers between devices: 8.83 us -> none  [partner_2(): return lax.ppermute(block, axis, route)]
  transfers between devices with their start and end apart: 10 -> 0, of which waited for: 6 -> 0; matrix products, arithmetic and copies ran while one was open for 8% -> 0% of each run, Pallas kernels for 0% -> 0%
where the time goes in v1:
time: 183 us; the launch traced here: 182 us
  Pallas kernels  165 us (90%)
  local copies, waits for them, and re-layouts  8.94 us (5%)
  other arithmetic  4.64 us (3%)
  between operations  2.22 us (1%)
    pallas_call x1, Pallas kernels, per_device(): pl.pallas_call(gather_kernel, out_shape=(jax.ShapeDtypeStruct((4, 4, 160,...  102 us
    pallas_call x1, Pallas kernels, per_device(): pl.pallas_call(tail_kernel, out_shape=jax.ShapeDtypeStruct((64, 512), F32...  47.5 us
    pallas_call x1, Pallas kernels, per_device(): pl.pallas_call(attention_kernel, out_shape=jax.ShapeDtypeStruct((2, 64, 5...  16.1 us

profile of v1, /device:TPU:6, one launch (start us, length us, event | category | flops | bytes accessed | tf_op | source)
XLA Modules:
  0.0 181.9 jit_solution(13990832917244228318)
XLA Ops:
  0.6 0.0 copy-start.1
  0.6 0.0 copy-start.2
  0.7 0.1 pad.44.clone
  0.7 1.0 maximum_bitcast_fusion
  1.8 0.7 pad.28
  2.5 0.8 pad.49
  3.3 0.9 copy.28
  4.2 0.7 fusion.4.w_in
  4.9 0.8 reshape.58
  5.8 0.1 reshape.59
  5.9 1.4 fusion.6.ow_in
  7.3 1.1 copy.29
  8.4 0.5 dot_general.8
  8.9 0.9 fusion
  9.8 0.1 copy.37
  9.9 0.1 reshape.77
  10.0 0.7 pad.33.mp
  10.7 101.7 %gather.1 = (bf16[4,4,160,640]{3,2,1,0:T(8,128)(2,1)}, bf16[2,4,4,80,640]{4,3,2,1,0:T(8,128)(2,1)}, bf16[2,4,16,64,256]{4,3,2,1,0:T(8,128)(2,1)}, f32[4,4,8,256]{3,2,1,0:T(8,128)}) custom-call(bf16[160,640]{1,0:T(8,128)(2,1)} %bitcast.33, bf16[80,640]{1,0:T(8,128)(2,1)} %fusion.4.w_in, bf16[64,256]{1,0:T(8,128)(2,1)} %fusion.6.ow_in, f32[16,8,256]{2,1,0:T(8,128)} %pad.33.mp), custom_call_target="tpu_custom_call" | custom-call | tf_op jit(solution)/shard_map/gather/pallas_call | solution.py:412
  112.4 0.0 copy-done.1
  112.4 0.0 copy-done.2
  112.4 0.1 copy.33
  112.5 0.6 pad.34.G
  113.1 16.1 %attention.1.att = bf16[2,64,512]{2,1,0:T(8,128)(2,1)} custom-call(bf16[16,160,640]{2,1,0:T(8,128)(2,1)} %bitcast.30, bf16[2560,640]{1,0:T(8,128)(2,1)} %bitcast.31, f32[16,8,256]{2,1,0:T(8,128)} %bitcast.35, f32[64,128]{1,0:T(8,128)} %pad.34.G, s32[16]{0:T(128)} %text_len.1), custom_call_target="tpu_custom_call" | custom-call | tf_op jit(solution)/shard_map/attention/pallas_call | solution.py:423
  129.2 0.0 copy-start.3
  129.2 0.0 copy-start
  129.2 47.5 %tail.1 = f32[64,512]{1,0:T(8,128)} custom-call(bf16[2,64,512]{2,1,0:T(8,128)(2,1)} %attention.1.att, bf16[4,4,160,640]{3,2,1,0:T(8,128)(2,1)} %get-tuple-element.6.X, f32[16,8,256]{2,1,0:T(8,128)} %bitcast.36, bf16[2,4,16,64,256]{4,3,2,1,0:T(8,128)(2,1)} %get-tuple-element.9.OW), custom_call_target="tpu_custom_call" | custom-call | tf_op jit(solution)/shard_map/tail/pallas_call | solution.py:433
  176.8 0.0 copy-done.3
  176.8 0.6 dynamic_slice.4
  178.8 0.0 copy-done
  178.8 1.6 multiply_add_fusion
  180.4 1.6 copy.43
  (9 shorter events, 0.2 us)
Async XLA Ops:
  0.6 111.7 %copy-start.1 = (f32[2,64]{1,0:T(2,128)S(1)}, f32[2,64]{1,0:T(2,128)}, u32[]{:S(2)}) copy-start(f32[2,64]{1,0:T(2,128)} %param.23) | copy-start | bytes 1540
  0.6 111.7 %copy-start.2 = (f32[64]{0:T(128)S(1)}, f32[64]{0:T(128)}, u32[]{:S(2)}) copy-start(f32[64]{0:T(128)} %param.22) | copy-start | bytes 772
  129.2 47.6 %copy-start.3 = (s32[16]{0:T(128)S(1)}, s32[16]{0:T(128)}, u32[]{:S(2)}) copy-start(s32[16]{0:T(128)} %param.16) | copy-start | bytes 196
  129.2 49.5 %copy-start = (f32[512,64]{0,1:T(8,128)S(1)}, f32[512,64]{0,1:T(8,128)}, u32[]{:S(2)}) copy-start(f32[512,64]{0,1:T(8,128)} %param.17) | copy-start | bytes 393220

commit v2 on v1

v2 whole, which is shorter than its diff:
```python
import jax
import jax.numpy as jnp
from jax import lax
from jax.experimental import pallas as pl
from jax.experimental.pallas import tpu as pltpu
from jax.sharding import PartitionSpec as P

STEPS = 28
EPS_NORM = 1e-06
WIDTH = 2432
MESH = pl.DeviceIdType.MESH
BF = jnp.bfloat16
F32 = jnp.float32
VMEM = pl.BlockSpec(memory_space=pltpu.VMEM)
SMEM = pl.BlockSpec(memory_space=pltpu.SMEM)


def place():
    r, c = lax.axis_index("row"), lax.axis_index("col")
    return r // 8, (r // 2) % 4, r % 2, c // 4, c % 4


def device(x, zl, core, y, zh):
    return ((x * 4 + zl) * 2 + core, y * 4 + zh)


def up(v, d, n=4):
    return lax.rem(v + d + n, n)


def meet(devices):
    barrier = pltpu.get_barrier_semaphore()
    for d in devices:
        pl.semaphore_signal(barrier, inc=1, device_id=d, device_id_type=MESH)
    pl.semaphore_wait(barrier, len(devices))


class Post:
    def __init__(self, send_sem, recv_sem):
        self.send_sem, self.recv_sem, self.n, self.sent = send_sem, recv_sem, 0, []

    def send(self, src, dst, to, got):
        k = self.n
        self.n += 1
        copy = pltpu.make_async_remote_copy(
            src_ref=src, dst_ref=dst, send_sem=self.send_sem.at[k], recv_sem=self.recv_sem.at[k],
            device_id=to, device_id_type=MESH)
        copy.start()
        self.sent.append(copy)
        back = pltpu.make_async_remote_copy(
            src_ref=got, dst_ref=got, send_sem=self.send_sem.at[k], recv_sem=self.recv_sem.at[k],
            device_id=to, device_id_type=MESH)
        return back.wait_recv

    def finish(self):
        for copy in self.sent:
            copy.wait_send()


def tdot(a, b):
    return lax.dot_general(a, b, (((0,), (0,)), ((), ())), preferred_element_type=F32)


def all_of(waits):
    for wait in waits:
        wait()


def block_kernel(h_in, t_in, qkv_in, kv_in, ow_in, fw_in, mw_in, cond, G, text_len, sigma, latent,
                 out, X, W, OW, FX, FW, mp, part, tot, M, W2, R, KB, VB, QC, AT, A, acc, U, ST, VP, VZ,
                 send_sem, recv_sem):
    x, zl, core, y, zh = place()
    me = x * 4 + zl
    zg = zh * 4 + zl

    def at_chip(q):
        return (q * 2 + core, y * 4 + zh)

    def at_x(d):
        return device(up(x, d), zl, core, y, zh)

    def at_y(d):
        return device(x, zl, core, up(y, d), zh)

    def at_zh(d):
        return device(x, zl, core, y, up(zh, d))

    def at_zl(d):
        return device(x, up(zl, d), core, y, zh)

    def at_z(d):
        z = up(zg, d, 16)
        return device(x, lax.rem(z, 4), core, y, z // 4)

    partner = device(x, zl, 1 - core, y, zh)
    X[y, zh, :, 0:512] = h_in[...]
    X[y, zh, :, 512:640] = jnp.concatenate([t_in[...], jnp.zeros((152, 32), BF)], axis=1)
    meet([at_chip(up(me, d, 16)) for d in range(1, 16)] + [at_zh(d) for d in (1, 2, 3)]
         + [at_y(d) for d in (1, 2, 3)] + [at_z(1), at_z(-1), partner])
    post = Post(send_sem, recv_sem)
    send = post.send
    lo, hi = pl.ds(0, 80), pl.ds(80, 72)

    def relay(a, to, got):
        return send(a, a, to, got)

    def z_out(ch):
        return (relay(X.at[y, zh, ch], at_zh(1), X.at[y, up(zh, -1), ch]),
                relay(X.at[y, zh, ch], at_zh(-1), X.at[y, up(zh, 1), ch]))

    class Rows:
        def __init__(self, z):
            self.z, self.got = z, {}

        def out(self, ch, name):
            z = self.z
            self.got[name] = (relay(X.at[y, z, ch], at_y(1), X.at[up(y, -1), z, ch]),
                              relay(X.at[y, z, ch], at_y(-1), X.at[up(y, 1), z, ch]))

        def on(self):
            z = self.z
            self.got["lo"][0]()
            f = relay(X.at[up(y, -1), z, lo], at_y(1), X.at[up(y, 2), z, lo])
            self.got["hi"][1]()
            g = relay(X.at[up(y, 1), z, hi], at_y(-1), X.at[up(y, 2), z, hi])
            self.rest = [self.got["hi"][0], self.got["lo"][1], f, g]

        def done(self):
            all_of(self.rest)

    zp_lo = relay(X.at[y, zh, lo], at_zh(1), X.at[y, up(zh, -1), lo])
    zm_hi = relay(X.at[y, zh, hi], at_zh(-1), X.at[y, up(zh, 1), hi])
    zp_hi = relay(X.at[y, zh, hi], at_zh(1), X.at[y, up(zh, -1), hi])
    zm_lo = relay(X.at[y, zh, lo], at_zh(-1), X.at[y, up(zh, 1), lo])
    rows = [Rows(zh), Rows(up(zh, -1)), Rows(up(zh, 1)), Rows(up(zh, 2))]
    rows[0].out(lo, "lo")
    rows[0].out(hi, "hi")

    c = cond[...]
    act = (c * jax.nn.sigmoid(c)).astype(BF)
    mp[...] = jnp.zeros_like(mp)
    for g in range(7):
        mp[:, g, 0:152] = lax.dot_general(act, mw_in[g], (((1,), (1,)), ((), ())), preferred_element_type=F32)
    mods = []
    for d in range(1, 16):
        q, p = up(me, d, 16), up(me, -d, 16)
        mods.append(send(mp.at[q], part.at[me], at_chip(q), part.at[p]))
    W[core, x, zl] = jnp.zeros((5, 80, 128), BF)
    W[core, x, zl, 0:3, 0:76] = qkv_in[...]
    W[core, x, zl, 3:5, 0:76] = kv_in[...]
    w_z = [relay(W.at[core, x, zl], at_zl(d), W.at[core, x, up(zl, -d)]) for d in (1, 3, 2)]
    FX[x] = jnp.concatenate([fw_in[...], jnp.zeros((64, 52), BF)], axis=1)
    f_x = [relay(FX.at[x], at_x(d), FX.at[up(x, -d)]) for d in (1, 3, 2)]
    o = ow_in[...]
    OW[core, x, zg, 0:64] = o[:, :128]
    OW[core, x, zg, 64:80] = jnp.concatenate(
        [o[16 * g:16 * g + 16, 128:152] for g in range(4)] + [jnp.zeros((16, 32), BF)], axis=1)

    part[me] = mp[me]
    all_of(mods)
    total = part[0]
    for i in range(1, 16):
        total = total + part[i]
    tot[core] = total
    tw = relay(tot.at[core], partner, tot.at[1 - core])
    rows[0].on()
    tw()
    M[y, zh] = tot[0] + tot[1]
    m_z = [relay(M.at[y, zh], at_zh(d), M.at[y, up(zh, -d)]) for d in (1, 3, 2)]
    all_of(f_x)
    FW[core, zl] = FX[y]
    f_z = [relay(FW.at[core, zl], at_zl(d), FW.at[core, up(zl, -d)]) for d in (1, 3, 2)]

    def x_out(ref):
        return (relay(ref.at[core, x], at_x(1), ref.at[core, up(x, -1)]),
                relay(ref.at[core, x], at_x(-1), ref.at[core, up(x, 1)]))

    def x_on(ref, waits, half):
        waits[0]()
        f = relay(ref.at[core, up(x, -1), pl.ds(0, half)], at_x(1), ref.at[core, up(x, 2), pl.ds(0, half)])
        waits[1]()
        g = relay(ref.at[core, up(x, 1), pl.ds(half, half)], at_x(-1), ref.at[core, up(x, 2), pl.ds(half, half)])
        return f, g

    def across(ref, d):
        return relay(ref.at[core, up(x, d)], partner, ref.at[1 - core, up(x, d)])

    zp_lo()
    zpf = relay(X.at[y, up(zh, -1), lo], at_zh(1), X.at[y, up(zh, 2), lo])
    rows[1].out(lo, "lo")
    zm_hi()
    zmf = relay(X.at[y, up(zh, 1), hi], at_zh(-1), X.at[y, up(zh, 2), hi])
    rows[2].out(hi, "hi")
    all_of(w_z)
    w_x = x_out(W)
    w_a = [across(W, 0)]
    all_of(m_z)
    m_y = [relay(M.at[y], at_y(d), M.at[up(y, -d)]) for d in (1, 3, 2)]
    zp_hi()
    rows[1].out(hi, "hi")
    zm_lo()
    rows[2].out(lo, "lo")
    rows[0].done()

    def tally(blocks, carry):
        s, q = carry
        for yy, zz in blocks:
            v = X[yy, zz].astype(F32)
            s = s + v.reshape(19, 8, 640).sum(axis=0)
            q = q + (v * v).reshape(19, 8, 640).sum(axis=0)
        return s, q

    def ys(z):
        return [(up(y, d), z) for d in range(4)]

    zero = jnp.zeros((8, 640), F32)
    stat = tally(ys(zh), (zero, zero))
    w_xf = x_on(W, w_x, 2)
    w_a += [across(W, -1), across(W, 1)]
    rows[1].on()
    rows[2].on()
    all_of(f_z)
    f_a = [relay(FW.at[core], partner, FW.at[1 - core])]
    zpf()
    rows[3].out(lo, "lo")
    zmf()
    rows[3].out(hi, "hi")

    def background():
        for s in range(1, 9):
            if s < 8:
                a, b = up(zg, 1 - s, 16), up(zg, s - 1, 16)
                step = (relay(OW.at[core, x, a], at_z(1), OW.at[core, x, up(zg, -s, 16)]),
                        relay(OW.at[core, x, b], at_z(-1), OW.at[core, x, up(zg, s, 16)]))
            else:
                t, u = pl.ds(0, 48), pl.ds(48, 32)
                e = up(zg, 8, 16)
                step = (relay(OW.at[core, x, up(zg, -7, 16), t], at_z(1), OW.at[core, x, e, t]),
                        relay(OW.at[core, x, up(zg, 7, 16), u], at_z(-1), OW.at[core, x, e, u]))
            yield
            all_of(step)
        o_x = x_out(OW)
        o_a = [across(OW, 0)]
        yield
        o_xf = x_on(OW, o_x, 8)
        o_a += [across(OW, -1), across(OW, 1)]
        yield
        all_of(o_xf)
        o_a.append(across(OW, 2))
        yield
        all_of(o_a)
        yield

    work = background()
    next(work)
    all_of(w_xf)
    w_a.append(across(W, 2))
    rows[1].done()
    rows[2].done()
    next(work)
    stat = tally(ys(up(zh, -1)) + ys(up(zh, 1)), stat)
    all_of(w_a)
    all_of(m_y)

    def join(i, carry):
        xx, ll = i // 4, lax.rem(i, 4)
        for g in range(5):
            a = W[0, xx, ll, g].astype(F32)
            b = W[1, xx, ll, g].astype(F32)
            w = jnp.concatenate([a[:76], b[:76], jnp.zeros((8, 128), F32)], axis=0)
            W2[pl.ds(pl.multiple_of(160 * i, 32), 160), 128 * g:128 * g + 128] = w.astype(BF)
        return carry

    lax.fori_loop(0, 16, join, 0)
    rows[3].on()
    next(work)
    rows[3].done()
    s, q = tally(ys(up(zh, 2)), stat)
    next(work)
    mean = jnp.sum(s, axis=0, keepdims=True) / WIDTH
    square = jnp.sum(q, axis=0, keepdims=True) / WIDTH
    rs = lax.rsqrt(square - mean * mean + EPS_NORM)

    def make_ready(i, carry):
        yy, zz = i // 4, lax.rem(i, 4)
        v = (X[yy, zz].astype(F32) - mean) * rs
        m = M[yy, zz].T
        a = v[:, :512] * (1.0 + m[:152, 1:2]) + m[:152, 0:1]
        b = v[:, 512:] * (1.0 + m[:152, 4:5]) + m[:152, 3:4]
        r = jnp.concatenate([jnp.concatenate([a, b], axis=1), jnp.zeros((8, 640), F32)], axis=0)
        R[pl.ds(pl.multiple_of(160 * i, 32), 160)] = r.astype(BF)
        return carry

    lax.fori_loop(0, 8, make_ready, 0)
    next(work)
    lax.fori_loop(8, 16, make_ready, 0)
    next(work)

    def normed(u, g):
        square = jnp.mean(u * u, axis=0, keepdims=True)
        return u * lax.rsqrt(square + EPS_NORM) * g

    def two(u, g):
        return jnp.concatenate([normed(u[:64], g), normed(u[64:], g)], axis=0)

    kv = tdot(W2[:, 128:384], R[:, :512])
    tkv = tdot(W2[:, 384:640], R[:, 512:])
    KB[0, :512] = two(kv[:128], G[:, 1:2]).T.astype(BF)
    KB[0, 512:] = two(tkv[:128], G[:, 2:3]).T.astype(BF)
    VB[0, :, :512] = kv[128:].astype(BF)
    VB[0, :, 512:] = tkv[128:].astype(BF)
    waits = [send(KB.at[0], KB.at[1], partner, KB.at[1]), send(VB.at[0], VB.at[1], partner, VB.at[1])]
    next(work)
    qt = two(tdot(W2[:, :128], R[:, :512]), G[:, 0:1])
    head = lax.broadcasted_iota(jnp.int32, (128, 512), 0) // 64
    qz = [jnp.where(head == h, qt, 0.0).astype(BF) for h in range(2)]
    for t in range(4):
        QC[t] = jnp.concatenate([qz[0][:, 128 * t:128 * t + 128], qz[1][:, 128 * t:128 * t + 128]], axis=1)
    next(work)
    all_of(waits)

    length = text_len[me]
    slot = lax.broadcasted_iota(jnp.int32, (128, 256), 0)
    valid = [(slot < 96) & (slot + 96 * owner < length) for owner in (core, 1 - core)]
    a_z = {}
    for d in (2, 1, 3, 0):
        t = QC[up(zh, d)]
        scores = []
        for j in range(2):
            sc = jnp.dot(KB[j], t, preferred_element_type=F32) * 0.125
            scores += [sc[:512], jnp.where(valid[j], sc[512:], -jnp.inf)]
        top = scores[0].max(axis=0, keepdims=True)
        for sc in scores[1:]:
            top = jnp.maximum(top, sc.max(axis=0, keepdims=True))
        e = [jnp.exp(sc - top) for sc in scores]
        total = sum(v.sum(axis=0, keepdims=True) for v in e)
        inv = 1.0 / total
        p = [(v * inv).astype(BF) for v in e]
        o = 0.0
        for j in range(2):
            o = o + jnp.dot(VB[j, :, :512], p[2 * j], preferred_element_type=F32)
            o = o + jnp.dot(VB[j, :, 512:], p[2 * j + 1], preferred_element_type=F32)
        if d:
            AT[d - 1, 0] = o[:64, :128].astype(BF)
            AT[d - 1, 1] = o[64:, 128:].astype(BF)
            a_z[d] = send(AT.at[d - 1], A.at[:, y, zh], at_zh(d), A.at[:, y, up(zh, -d)])
        else:
            A[0, y, zh] = o[:64, :128].astype(BF)
            A[1, y, zh] = o[64:, 128:].astype(BF)
        next(work)

    a_y = []

    def along_y(z):
        for e in (1, 3, 2):
            a_y.append(relay(A.at[:, y, z], at_y(e), A.at[:, up(y, -e), z]))

    along_y(zh)
    for d in (1, 3, 2):
        a_z[d]()
        along_y(up(zh, -d))
    for _ in work:
        pass

    def project(yy, first):
        for z in range(4):
            t = 0.0
            for h in range(2):
                a = A[h, yy].reshape(256, 128)
                w = OW[h, yy, 4 * z:4 * z + 4]
                tail = jnp.concatenate([w[:, 64:80, 24 * g:24 * g + 24] for g in range(4)], axis=1)
                w = jnp.concatenate([w[:, :64], tail], axis=2).reshape(256, 152)
                t = t + tdot(a, w)
            acc[z] = t if first else acc[z] + t

    project(y, True)
    for k, e in enumerate((1, 3, 2)):
        all_of(a_y[k::3])
        project(up(y, -e), False)
    s = q = jnp.zeros((8, 128), F32)
    mine = pl.ds(pl.multiple_of(128 * zh, 128), 128)
    for z in range(4):
        m = M[y, z].T
        u = (X[y, z, :, mine].astype(F32) + m[:152, 2:3] * acc[z].T).astype(BF)
        U[z] = u
        v = u.astype(F32)
        s = s + v.reshape(19, 8, 128).sum(axis=0)
        q = q + (v * v).reshape(19, 8, 128).sum(axis=0)
    ST[y, 0] = s
    ST[y, 1] = q
    all_of([relay(ST.at[y], at_y(d), ST.at[up(y, -d)]) for d in (1, 3, 2)])
    all_of(f_a)
    st = ST[0] + ST[1] + (ST[2] + ST[3])
    mean = jnp.sum(st[0], axis=0, keepdims=True) / WIDTH
    square = jnp.sum(st[1], axis=0, keepdims=True) / WIDTH
    rs = lax.rsqrt(square - mean * mean + EPS_NORM)
    vel = 0.0
    for z in range(4):
        m = M[y, z].T
        head_in = ((U[z].astype(F32) - mean) * rs) * (1.0 + m[:152, 6:7]) + m[:152, 5:6]
        for h in range(2):
            vel = vel + jnp.dot(FW[h, z][:, :76], head_in[76 * h:76 * h + 76].astype(BF),
                                preferred_element_type=F32)
    VP[y] = vel
    all_of([relay(VP.at[y], at_y(d), VP.at[up(y, -d)]) for d in (1, 3, 2)])
    VZ[zh] = VP[0] + VP[1] + (VP[2] + VP[3])
    all_of([relay(VZ.at[zh], at_zh(d), VZ.at[up(zh, -d)]) for d in (1, 3, 2)])
    step = sigma[me]
    for z in range(4):
        v = VZ[z]
        out[0, :, 128 * z:128 * z + 128] = v
        out[1, :, 128 * z:128 * z + 128] = latent[:, 128 * z:128 * z + 128] + step * v
    post.finish()


def sigma_of(step_now):
    remain = 1.0 - step_now.astype(F32) / STEPS
    return 3.0 * remain / (1.0 + 2.0 * remain)


def dma(n):
    return pltpu.SemaphoreType.DMA((n,))


SCRATCH = [
    ((4, 4, 152, 640), BF),
    ((2, 4, 4, 5, 80, 128), BF),
    ((2, 4, 16, 80, 128), BF),
    ((4, 64, 128), BF),
    ((2, 4, 64, 128), BF),
    ((16, 8, 256), F32),
    ((16, 8, 256), F32),
    ((2, 8, 256), F32),
    ((4, 4, 8, 256), F32),
    ((2560, 640), BF),
    ((2560, 640), BF),
    ((2, 640, 128), BF),
    ((2, 128, 640), BF),
    ((4, 128, 256), BF),
    ((3, 2, 64, 128), BF),
    ((2, 4, 4, 64, 128), BF),
    ((4, 128, 152), F32),
    ((4, 152, 128), BF),
    ((4, 2, 8, 128), F32),
    ((4, 64, 128), F32),
    ((4, 64, 128), F32),
]


def per_device(hidden_img, hidden_txt, text_len, step_index, latent, cond, mod_weight, qkv_weight,
               kv_text_weight, q_gain, k_gain, out_weight, final_weight):
    gains = jnp.stack([q_gain, k_gain[0], k_gain[1]], axis=1)
    sigma = sigma_of(step_index + 1) - sigma_of(step_index)
    out = pl.pallas_call(
        block_kernel,
        out_shape=jax.ShapeDtypeStruct((2, 64, 512), F32),
        in_specs=[VMEM] * 9 + [SMEM, SMEM, VMEM],
        out_specs=VMEM,
        scratch_shapes=[pltpu.VMEM(s, t) for s, t in SCRATCH] + [dma(160), dma(160)],
        compiler_params=pltpu.CompilerParams(collective_id=0, has_side_effects=True, vmem_limit_bytes=60 << 20),
        name="block",
    )(hidden_img.T, hidden_txt.T, qkv_weight.transpose(1, 0, 2), kv_text_weight.transpose(1, 0, 2), out_weight,
      final_weight.T, mod_weight.transpose(1, 2, 0), cond, gains, text_len, sigma, latent.T)
    return out[0].T, out[1].T


def solution(mesh):
    in_specs = (P("row", "col"), P("row", "col"), P(), P(), P("row", None), P(None, "row"),
                P("row", None, "col"), P("row", None, "col"), P("row", None, "col"), P(), P(),
                P("row", "col"), P("row", None))
    out_specs = (P("row", None), P("row", None))
    return jax.shard_map(per_device, mesh=mesh, in_specs=in_specs, out_specs=out_specs, check_vma=False)
```

time: 183 us -> 147 us (0.80)
  Pallas kernels: 165 us -> 140 us
  local copies, waits for them, and re-layouts: 8.94 us -> 3.78 us
  other arithmetic: 4.64 us -> 2 us
    pallas_call x3 -> x1, Pallas kernels: 165 us -> 140 us  [per_device(): pl.pallas_call(block_kernel, out_shape=jax.ShapeDtypeStruct((2, 64, 512),...]
    unnamed x15 -> x3, local copies, waits for them, and re-layouts: 3.38 us -> 0.63 us
    reshape x5 -> x0, local copies, waits for them, and re-layouts: 2.25 us -> none  [the longest x1 1.15 us: per_device(): mod_weight.reshape(76, 7 * 152)]
    pad x5 -> x0, local copies, waits for them, and re-layouts: 2.08 us -> none  [the longest x3 0.79 us: split80(): return jnp.pad(v, pads).reshape(shape[:axis] + (160,) + shape[axis + 1:])]
    concatenate x2 -> x0, other arithmetic: 2.07 us -> none  [the longest x1 1.42 us: per_device(): jnp.concatenate([split80(out_weight, 1), jnp.pad(final_weight.T, ((0, 0),...]
where the time goes in v2:
time: 147 us
  Pallas kernels  140 us (95%)
  local copies, waits for them, and re-layouts  3.78 us (3%)
  other arithmetic  2 us (1%)
    pallas_call x1, Pallas kernels, per_device(): pl.pallas_call(block_kernel, out_shape=jax.ShapeDtypeStruct((2, 64, 512),...  140 us

profile of v2, /device:TPU:6, one launch (start us, length us, event | category | flops | bytes accessed | tf_op | source)
XLA Modules:
  0.0 146.8 jit_solution(16193564150063858613)
XLA Ops:
  0.6 0.0 copy-start
  0.6 1.3 divide_subtract_fusion.sigma
  2.0 0.8 slice_bitcast_fusion.3
  2.7 0.7 pad_maximum_fusion
  3.4 0.7 copy.20.G
  4.1 0.0 copy-done
  4.1 0.6 copy.22
  4.7 140.3 %block.1 = f32[2,64,512]{2,1,0:T(8,128)} custom-call(bf16[152,512]{1,0:T(8,128)(2,1)} %bitcast.24, bf16[152,96]{1,0:T(8,128)(2,1)} %bitcast.27, bf16[3,76,128]{2,1,0:T(8,128)(2,1)} %bitcast.26, bf16[2,76,128]{2,1,0:T(8,128)(2,1)} %bitcast.23, bf16[64,152]{1,0:T(8,128)(2,1)} %ow_in.1, bf16[64,76]{1,0:T(8,128)(2,1)} %bitcast.28, bf16[7,152,76]{2,1,0:T(8,128)(2,1)} %bitcast.22, ...), custom_call_target="tpu_custom_call" | custom-call | tf_op jit(solution)/shard_map/block/pallas_call | solution.py:454
  145.1 1.7 %slice_bitcast_fusion = (f32[512,64]{0,1:T(8,128)}, f32[512,64]{0,1:T(8,128)}) fusion(f32[2,64,512]{2,1,0:T(8,128)} %block.1), kind=kLoop, calls=%fused_computation | loop fusion | bytes 524288 | tf_op jit(solution)/shard_map/transpose | solution.py:464
Async XLA Ops:
  0.6 3.5 %copy-start = (bf16[76,2,128]{2,1,0:T(2,128)(2,1)S(1)}, bf16[76,2,128]{2,1,0:T(2,128)(2,1)}, u32[]{:S(2)}) copy-start(bf16[76,2,128]{2,1,0:T(2,128)(2,1)} %param.21) | copy-start | bytes 116740

commit v3 on v2

v3 whole, which is shorter than its diff:
```python
import jax
import jax.numpy as jnp
from jax import lax
from jax.experimental import pallas as pl
from jax.experimental.pallas import tpu as pltpu
from jax.sharding import PartitionSpec as P

STEPS = 28
EPS_NORM = 1e-06
WIDTH = 2432
MESH = pl.DeviceIdType.MESH
BF = jnp.bfloat16
F32 = jnp.float32
VMEM = pl.BlockSpec(memory_space=pltpu.VMEM)
SMEM = pl.BlockSpec(memory_space=pltpu.SMEM)


def place():
    r, c = lax.axis_index("row"), lax.axis_index("col")
    return r // 8, (r // 2) % 4, r % 2, c // 4, c % 4


def device(x, zl, core, y, zh):
    return ((x * 4 + zl) * 2 + core, y * 4 + zh)


def up(v, d, n=4):
    return lax.rem(v + d + n, n)


def sigma_of(step_now):
    remain = 1.0 - step_now.astype(F32) / STEPS
    return 3.0 * remain / (1.0 + 2.0 * remain)


class Post:
    def __init__(self, send_sem, recv_sem):
        self.send_sem, self.recv_sem, self.n, self.sent, self.todo = send_sem, recv_sem, 0, [], []

    def send(self, src, dst, to, got):
        k = self.n
        self.n += 1
        copy = pltpu.make_async_remote_copy(
            src_ref=src, dst_ref=dst, send_sem=self.send_sem.at[k], recv_sem=self.recv_sem.at[k],
            device_id=to, device_id_type=MESH)
        copy.start()
        self.sent.append(copy)
        back = pltpu.make_async_remote_copy(
            src_ref=got, dst_ref=got, send_sem=self.send_sem.at[k], recv_sem=self.recv_sem.at[k],
            device_id=to, device_id_type=MESH)
        todo = [True]
        self.todo.append((todo, back.wait_recv))

        def wait():
            assert todo[0]
            todo[0] = False
            back.wait_recv()
        return wait

    def finish(self):
        for copy in self.sent:
            copy.wait_send()


def drain(post):
    for todo, wait in post.todo:
        if todo[0]:
            wait()
    post.finish()


def tdot(a, b):
    return lax.dot_general(a, b, (((0,), (0,)), ((), ())), preferred_element_type=F32)


def all_of(waits):
    for wait in waits:
        wait()


def block_kernel(h_in, t_in, qkv_in, kv_in, ow_in, fw_in, mw_in, cond, qg, kg, text_len, step_index, latent,
                 out, X, W, OW, FX, FW, SS, mp, mx, ms, ml, tot, M, W2, R, PI, PT, KB, VB, QC, AT, A, acc, U, ST, VP, VZ,
                 send_sem, recv_sem):
    x, zl, core, y, zh = place()
    me = x * 4 + zl

    def at_x(d):
        return device(up(x, d), zl, core, y, zh)

    def at_y(d):
        return device(x, zl, core, up(y, d), zh)

    def at_zh(d):
        return device(x, zl, core, y, up(zh, d))

    def at_zl(d):
        return device(x, up(zl, d), core, y, zh)

    partner = device(x, zl, 1 - core, y, zh)
    three = (1, 3, 2)
    peers = [f(d) for f in (at_x, at_y, at_zh, at_zl) for d in three] + [partner]
    barrier = pltpu.get_barrier_semaphore()
    for p in peers:
        pl.semaphore_signal(barrier, inc=1, device_id=p, device_id_type=MESH)

    own = jnp.concatenate([h_in[...], jnp.concatenate([t_in[...], jnp.zeros((152, 32), BF)], axis=1)], axis=1)
    X[y, zh] = own
    v = own.astype(F32)
    SS[y, zh] = jnp.concatenate([jnp.sum(v, axis=0, keepdims=True), jnp.sum(v * v, axis=0, keepdims=True)], axis=0)
    W[core, x, zl] = jnp.zeros((5, 80, 128), BF)
    W[core, x, zl, 0:3, 0:76] = qkv_in[...]
    W[core, x, zl, 3:5, 0:76] = kv_in[...]
    FX[x] = jnp.concatenate([fw_in[...], jnp.zeros((64, 52), BF)], axis=1)
    o = ow_in[...]
    OW[core, x, zh, zl, 0:64] = o[:, :128]
    OW[core, x, zh, zl, 64:80] = jnp.concatenate(
        [o[16 * g:16 * g + 16, 128:152] for g in range(4)] + [jnp.zeros((16, 32), BF)], axis=1)
    mp[...] = jnp.zeros_like(mp)
    pl.semaphore_wait(barrier, len(peers))

    post = Post(send_sem, recv_sem)
    send = post.send
    lo, hi = pl.ds(0, 80), pl.ds(80, 72)

    def relay(a, to, got):
        return send(a, a, to, got)

    class Rows:
        def __init__(self, z):
            self.z, self.got = z, {}

        def out(self, ch, name):
            z = self.z
            self.got[name] = (relay(X.at[y, z, ch], at_y(1), X.at[up(y, -1), z, ch]),
                              relay(X.at[y, z, ch], at_y(-1), X.at[up(y, 1), z, ch]))

        def on(self):
            z = self.z
            self.got["lo"][0]()
            f = relay(X.at[up(y, -1), z, lo], at_y(1), X.at[up(y, 2), z, lo])
            self.got["hi"][1]()
            g = relay(X.at[up(y, 1), z, hi], at_y(-1), X.at[up(y, 2), z, hi])
            self.rest = [self.got["hi"][0], self.got["lo"][1], f, g]

        def done(self):
            all_of(self.rest)

    rows = [Rows(zh), Rows(up(zh, -1)), Rows(up(zh, 1)), Rows(up(zh, 2))]
    ss_z = [relay(SS.at[y, zh], at_zh(d), SS.at[y, up(zh, -d)]) for d in three]
    rows[0].out(lo, "lo")
    rows[0].out(hi, "hi")
    w_z = [relay(W.at[core, x, zl], at_zl(d), W.at[core, x, up(zl, -d)]) for d in three]
    zp_lo = relay(X.at[y, zh, lo], at_zh(1), X.at[y, up(zh, -1), lo])
    zm_hi = relay(X.at[y, zh, hi], at_zh(-1), X.at[y, up(zh, 1), hi])

    c = cond[...]
    act = (c * jax.nn.sigmoid(c)).astype(BF)
    for g in range(7):
        t = lax.dot_general(act, mw_in[g], (((1,), (1,)), ((), ())), preferred_element_type=F32)
        for i in range(4):
            mp[i, :, g, 0:152] = t[4 * i:4 * i + 4]
    mods = [send(mp.at[up(x, d)], mx.at[x], at_x(d), mx.at[up(x, -d)]) for d in three]
    f_x = [relay(FX.at[x], at_x(d), FX.at[up(x, -d)]) for d in three]
    mx[x] = mp[x]
    all_of(mods)
    ms[...] = (mx[0] + mx[1]) + (mx[2] + mx[3])
    mods = [send(ms.at[up(zl, d)], ml.at[zl], at_zl(d), ml.at[up(zl, -d)]) for d in three]
    zp_hi = relay(X.at[y, zh, hi], at_zh(1), X.at[y, up(zh, -1), hi])
    zm_lo = relay(X.at[y, zh, lo], at_zh(-1), X.at[y, up(zh, 1), lo])
    all_of(ss_z)
    ss_y = [relay(SS.at[y], at_y(d), SS.at[up(y, -d)]) for d in three]
    ml[zl] = ms[zl]

    def x_out(part):
        a = part(x)
        return relay(a, at_x(1), part(up(x, -1))), relay(a, at_x(-1), part(up(x, 1)))

    def x_on(part, waits):
        waits[0]()
        t, u = pl.ds(0, 2), pl.ds(2, 2)
        f = relay(part(up(x, -1)).at[t], at_x(1), part(up(x, 2)).at[t])
        waits[1]()
        g = relay(part(up(x, 1)).at[u], at_x(-1), part(up(x, 2)).at[u])
        return f, g

    def w_part(i):
        return W.at[core, i]

    def across(d):
        return relay(W.at[core, up(x, d)], partner, W.at[1 - core, up(x, d)])

    rows[0].on()
    all_of(w_z)
    w_x = x_out(w_part)
    w_a = [across(0)]
    zp_lo()
    rows[1].out(lo, "lo")
    zm_hi()
    rows[2].out(hi, "hi")
    all_of(mods)
    tot[core] = (ml[0] + ml[1]) + (ml[2] + ml[3])
    tw = relay(tot.at[core], partner, tot.at[1 - core])
    all_of(ss_y)
    s = jnp.zeros((2, 640), F32)
    for i in range(16):
        s = s + SS[i // 4, i % 4]
    s = s / WIDTH
    mean = s[0:1]
    rs = lax.rsqrt(s[1:2] - mean * mean + EPS_NORM)
    tw()
    M[y, zh] = tot[0] + tot[1]
    m_z = [relay(M.at[y, zh], at_zh(d), M.at[y, up(zh, -d)]) for d in three]
    zpf = relay(X.at[y, up(zh, -1), lo], at_zh(1), X.at[y, up(zh, 2), lo])
    zmf = relay(X.at[y, up(zh, 1), hi], at_zh(-1), X.at[y, up(zh, 2), hi])
    all_of(f_x)
    FW[core, zl] = FX[y]
    o_l = [relay(OW.at[core, x, zh, zl], at_zl(d), OW.at[core, x, zh, up(zl, -d)]) for d in three]
    f_z = [relay(FW.at[core, zl], at_zl(d), FW.at[core, up(zl, -d)]) for d in three]
    w_xf = x_on(w_part, w_x)
    w_a += [across(-1), across(1)]
    zp_hi()
    rows[1].out(hi, "hi")
    zm_lo()
    rows[2].out(lo, "lo")
    rows[0].done()
    all_of(w_xf)
    w_a.append(across(2))
    rows[1].on()
    rows[2].on()
    all_of(w_a)
    all_of(m_z)
    m_y = [relay(M.at[y], at_y(d), M.at[up(y, -d)]) for d in three]

    def join(i, carry):
        xx, ll = lax.rem(i, 4), up(zh, i // 4)
        for g in range(5):
            a = W[0, xx, ll, g].astype(F32)
            b = W[1, xx, ll, g].astype(F32)
            w = jnp.concatenate([a[:76], b[:76], jnp.zeros((8, 128), F32)], axis=0)
            W2[pl.ds(pl.multiple_of(160 * i, 32), 160), 128 * g:128 * g + 128] = w.astype(BF)
        return carry

    lax.fori_loop(0, 16, join, 0)
    all_of(m_y)

    def ready(k):
        def one(i, carry):
            yy, zz = i, up(zh, k)
            v = (X[yy, zz].astype(F32) - mean) * rs
            m = M[yy, zz].T
            a = v[:, :512] * (1.0 + m[:152, 1:2]) + m[:152, 0:1]
            b = v[:, 512:] * (1.0 + m[:152, 4:5]) + m[:152, 3:4]
            r = jnp.concatenate([jnp.concatenate([a, b], axis=1), jnp.zeros((8, 640), F32)], axis=0)
            R[pl.ds(pl.multiple_of(640 * k + 160 * i, 32), 160)] = r.astype(BF)
            return carry

        lax.fori_loop(0, 4, one, 0)

    def dots(k, a, b, image):
        n = 640 * k
        lanes = slice(0, 512) if image else slice(512, 640)
        return tdot(W2[n:n + 640, a:b], R[n:n + 640, lanes])

    ready(0)
    PI[...] = dots(0, 0, 384, True)
    PT[...] = dots(0, 384, 640, False)
    zpf()
    rows[3].out(lo, "lo")
    zmf()
    rows[3].out(hi, "hi")

    def o_part(d):
        return lambda i: OW.at[core, i, up(zh, d)]

    def o_across(d):
        z = up(zh, d)
        return relay(OW.at[core, :, z], partner, OW.at[1 - core, :, z])

    def background():
        all_of(o_l)
        a, t, u = OW.at[core, x], pl.ds(0, 2), pl.ds(2, 2)
        zp = relay(a.at[zh], at_zh(1), a.at[up(zh, -1)])
        zm = relay(a.at[zh], at_zh(-1), a.at[up(zh, 1)])
        x0 = x_out(o_part(0))
        yield
        x0 = x_on(o_part(0), x0)
        yield
        zp()
        zpf = relay(a.at[up(zh, -1), t], at_zh(1), a.at[up(zh, 2), t])
        x3 = x_out(o_part(-1))
        zm()
        zmf = relay(a.at[up(zh, 1), u], at_zh(-1), a.at[up(zh, 2), u])
        x1 = x_out(o_part(1))
        all_of(x0)
        last = [o_across(0)]
        yield
        x3 = x_on(o_part(-1), x3)
        x1 = x_on(o_part(1), x1)
        yield
        zpf()
        zmf()
        x2 = x_out(o_part(2))
        all_of(x3)
        last.append(o_across(-1))
        all_of(x1)
        last.append(o_across(1))
        yield
        x2 = x_on(o_part(2), x2)
        yield
        all_of(x2)
        last.append(o_across(2))
        yield
        all_of(last)
        yield

    work = background()
    all_of(f_z)
    f_a = [relay(FW.at[core], partner, FW.at[1 - core])]
    next(work)
    rows[1].done()
    ready(3)
    PI[...] += dots(3, 0, 384, True)
    PT[...] += dots(3, 384, 640, False)
    rows[2].done()
    ready(1)
    PI[...] += dots(1, 0, 384, True)
    PT[...] += dots(1, 384, 640, False)
    rows[3].on()
    next(work)
    rows[3].done()
    ready(2)

    def normed(u, g):
        square = jnp.mean(u * u, axis=0, keepdims=True)
        return u * lax.rsqrt(square + EPS_NORM) * g

    def two(u, g):
        return jnp.concatenate([normed(u[:64], g), normed(u[64:], g)], axis=0)

    G = jnp.concatenate([qg[...], kg[...], jnp.zeros((5, 64), F32)], axis=0)
    G = jnp.concatenate([G, G], axis=1).T[:64]
    kv = PI[128:384] + dots(2, 128, 384, True)
    tkv = PT[...] + dots(2, 384, 640, False)
    KB[0, :512] = two(kv[:128], G[:, 1:2]).T.astype(BF)
    KB[0, 512:] = two(tkv[:128], G[:, 2:3]).T.astype(BF)
    VB[0, :, :512] = kv[128:].astype(BF)
    VB[0, :, 512:] = tkv[128:].astype(BF)
    waits = [send(KB.at[0], KB.at[1], partner, KB.at[1]), send(VB.at[0], VB.at[1], partner, VB.at[1])]
    qt = two(PI[0:128] + dots(2, 0, 128, True), G[:, 0:1])
    head = lax.broadcasted_iota(jnp.int32, (128, 512), 0) // 64
    qz = [jnp.where(head == h, qt, 0.0).astype(BF) for h in range(2)]
    for t in range(4):
        QC[t] = jnp.concatenate([qz[0][:, 128 * t:128 * t + 128], qz[1][:, 128 * t:128 * t + 128]], axis=1)
    next(work)
    all_of(waits)

    length = text_len[me]
    slot = lax.broadcasted_iota(jnp.int32, (128, 256), 0)
    valid = [(slot < 96) & (slot + 96 * owner < length) for owner in (core, 1 - core)]
    a_z = {}
    for d in (2, 1, 3, 0):
        t = QC[up(zh, d)]
        scores = []
        for j in range(2):
            sc = jnp.dot(KB[j], t, preferred_element_type=F32) * 0.125
            scores += [sc[:512], jnp.where(valid[j], sc[512:], -jnp.inf)]
        top = scores[0].max(axis=0, keepdims=True)
        for sc in scores[1:]:
            top = jnp.maximum(top, sc.max(axis=0, keepdims=True))
        e = [jnp.exp(sc - top) for sc in scores]
        total = sum(v.sum(axis=0, keepdims=True) for v in e)
        inv = 1.0 / total
        p = [(v * inv).astype(BF) for v in e]
        o = 0.0
        for j in range(2):
            o = o + jnp.dot(VB[j, :, :512], p[2 * j], preferred_element_type=F32)
            o = o + jnp.dot(VB[j, :, 512:], p[2 * j + 1], preferred_element_type=F32)
        if d:
            AT[d - 1, 0] = o[:64, :128].astype(BF)
            AT[d - 1, 1] = o[64:, 128:].astype(BF)
            a_z[d] = send(AT.at[d - 1], A.at[:, y, zh], at_zh(d), A.at[:, y, up(zh, -d)])
        else:
            A[0, y, zh] = o[:64, :128].astype(BF)
            A[1, y, zh] = o[64:, 128:].astype(BF)
        next(work)

    a_y = []

    def along_y(z):
        for e in (1, 3, 2):
            a_y.append(relay(A.at[:, y, z], at_y(e), A.at[:, up(y, -e), z]))

    along_y(zh)
    for d in (1, 3, 2):
        a_z[d]()
        along_y(up(zh, -d))
    for _ in work:
        pass

    def project(yy, first):
        for z in range(4):
            t = 0.0
            for h in range(2):
                a = A[h, yy].reshape(256, 128)
                w = OW[h, yy, z]
                tail = jnp.concatenate([w[:, 64:80, 24 * g:24 * g + 24] for g in range(4)], axis=1)
                w = jnp.concatenate([w[:, :64], tail], axis=2).reshape(256, 152)
                t = t + tdot(a, w)
            acc[z] = t if first else acc[z] + t

    project(y, True)
    for k, e in enumerate((1, 3, 2)):
        all_of(a_y[k::3])
        project(up(y, -e), False)
    s = q = jnp.zeros((8, 128), F32)
    mine = pl.ds(pl.multiple_of(128 * zh, 128), 128)
    for z in range(4):
        m = M[y, z].T
        u = (X[y, z, :, mine].astype(F32) + m[:152, 2:3] * acc[z].T).astype(BF)
        U[z] = u
        v = u.astype(F32)
        s = s + v.reshape(19, 8, 128).sum(axis=0)
        q = q + (v * v).reshape(19, 8, 128).sum(axis=0)
    ST[y, 0] = s
    ST[y, 1] = q
    all_of([relay(ST.at[y], at_y(d), ST.at[up(y, -d)]) for d in (1, 3, 2)])
    all_of(f_a)
    st = ST[0] + ST[1] + (ST[2] + ST[3])
    mean = jnp.sum(st[0], axis=0, keepdims=True) / WIDTH
    square = jnp.sum(st[1], axis=0, keepdims=True) / WIDTH
    rs = lax.rsqrt(square - mean * mean + EPS_NORM)
    vel = 0.0
    for z in range(4):
        m = M[y, z].T
        head_in = ((U[z].astype(F32) - mean) * rs) * (1.0 + m[:152, 6:7]) + m[:152, 5:6]
        for h in range(2):
            vel = vel + jnp.dot(FW[h, z][:, :76], head_in[76 * h:76 * h + 76].astype(BF),
                                preferred_element_type=F32)
    VP[y] = vel
    all_of([relay(VP.at[y], at_y(d), VP.at[up(y, -d)]) for d in (1, 3, 2)])
    VZ[zh] = (VP[0] + VP[1] + (VP[2] + VP[3])).astype(BF)
    all_of([relay(VZ.at[zh], at_zh(d), VZ.at[up(zh, -d)]) for d in (1, 3, 2)])
    now = jnp.full((8, 128), step_index[me], jnp.int32)
    step = (sigma_of(now + 1) - sigma_of(now))[0:1]
    for z in range(4):
        v = VZ[z].astype(F32)
        out[0, :, 128 * z:128 * z + 128] = v
        out[1, :, 128 * z:128 * z + 128] = latent[:, 128 * z:128 * z + 128] + step * v
    post.finish()


def dma(n):
    return pltpu.SemaphoreType.DMA((n,))


SCRATCH = [
    ((4, 4, 152, 640), BF),
    ((2, 4, 4, 5, 80, 128), BF),
    ((2, 4, 4, 4, 80, 128), BF),
    ((4, 64, 128), BF),
    ((2, 4, 64, 128), BF),
    ((4, 4, 2, 640), F32),
    ((4, 4, 8, 256), F32),
    ((4, 4, 8, 256), F32),
    ((4, 8, 256), F32),
    ((4, 8, 256), F32),
    ((2, 8, 256), F32),
    ((4, 4, 8, 256), F32),
    ((2560, 640), BF),
    ((2560, 640), BF),
    ((384, 512), F32),
    ((256, 128), F32),
    ((2, 640, 128), BF),
    ((2, 128, 640), BF),
    ((4, 128, 256), BF),
    ((3, 2, 64, 128), BF),
    ((2, 4, 4, 64, 128), BF),
    ((4, 128, 152), F32),
    ((4, 152, 128), BF),
    ((4, 2, 8, 128), F32),
    ((4, 64, 128), F32),
    ((4, 64, 128), BF),
]


def per_device(hidden_img, hidden_txt, text_len, step_index, latent, cond, mod_weight, qkv_weight,
               kv_text_weight, q_gain, k_gain, out_weight, final_weight):
    out = pl.pallas_call(
        block_kernel,
        out_shape=jax.ShapeDtypeStruct((2, 64, 512), F32),
        in_specs=[VMEM] * 10 + [SMEM, SMEM, VMEM],
        out_specs=VMEM,
        scratch_shapes=[pltpu.VMEM(s, t) for s, t in SCRATCH] + [dma(160), dma(160)],
        compiler_params=pltpu.CompilerParams(collective_id=0, has_side_effects=True, vmem_limit_bytes=60 << 20),
        name="block",
    )(hidden_img.T, hidden_txt.T, qkv_weight.transpose(1, 0, 2), kv_text_weight.transpose(1, 0, 2), out_weight,
      final_weight.T, mod_weight.transpose(1, 2, 0), cond, q_gain.reshape(1, 64), k_gain, text_len, step_index, latent.T)
    return out[0].T, out[1].T


def solution(mesh):
    in_specs = (P("row", "col"), P("row", "col"), P(), P(), P("row", None), P(None, "row"),
                P("row", None, "col"), P("row", None, "col"), P("row", None, "col"), P(), P(),
                P("row", "col"), P("row", None))
    out_specs = (P("row", None), P("row", None))
    return jax.shard_map(per_device, mesh=mesh, in_specs=in_specs, out_specs=out_specs, check_vma=False)
```

time: 147 us -> 122 us (0.83)
  Pallas kernels: 140 us -> 118 us
  other arithmetic: 2 us -> 0 us
    pallas_call x1, Pallas kernels: 140 us -> 118 us  [per_device(): pl.pallas_call(block_kernel, out_shape=jax.ShapeDtypeStruct((2, 64, 512),...]
where the time goes in v3:
time: 122 us
  Pallas kernels  118 us (97%)
  local copies, waits for them, and re-layouts  3.08 us (3%)
    pallas_call x1, Pallas kernels, per_device(): pl.pallas_call(block_kernel, out_shape=jax.ShapeDtypeStruct((2, 64, 512),...  118 us

profile of v3, /device:TPU:6, one launch (start us, length us, event | category | flops | bytes accessed | tf_op | source)
XLA Modules:
  0.0 121.6 jit_solution(10294681101617878215)
XLA Ops:
  0.6 1.4 %copy.17 = bf16[76,2,128]{2,0,1:T(8,128)(2,1)} copy(bf16[76,2,128]{2,1,0:T(2,128)(2,1)} %param.21) | data formatting | bytes 77824 | tf_op args[8]
  2.0 117.9 %block.1 = f32[2,64,512]{2,1,0:T(8,128)} custom-call(bf16[152,512]{1,0:T(8,128)(2,1)} %bitcast.20, bf16[152,96]{1,0:T(8,128)(2,1)} %bitcast.23, bf16[3,76,128]{2,1,0:T(8,128)(2,1)} %bitcast.22, bf16[2,76,128]{2,1,0:T(8,128)(2,1)} %bitcast.19, bf16[64,152]{1,0:T(8,128)(2,1)} %ow_in.1, bf16[64,76]{1,0:T(8,128)(2,1)} %bitcast.24, bf16[7,152,76]{2,1,0:T(8,128)(2,1)} %bitcast.18, ...), custom_call_target="tpu_custom_call" | custom-call | tf_op jit(solution)/shard_map/block/pallas_call | solution.py:488
  120.0 1.7 %slice_bitcast_fusion = (f32[512,64]{0,1:T(8,128)}, f32[512,64]{0,1:T(8,128)}) fusion(f32[2,64,512]{2,1,0:T(8,128)} %block.1), kind=kLoop, calls=%fused_computation | loop fusion | bytes 524288 | tf_op jit(solution)/shard_map/transpose | solution.py:498

commit v4 on v3

--- a/solution.py
+++ b/solution.py
@@ -98,7 +98,7 @@
 
     partner = device(x, zl, 1 - core, y, zh)
     three = (1, 3, 2)
-    peers = [f(d) for f in (at_x, at_y, at_zh, at_zl) for d in three] + [partner]
+    peers = [f(d) for f in (at_x, at_y, at_zl) for d in three] + [at_zh(1), at_zh(-1), partner]
     barrier = pltpu.get_barrier_semaphore()
     for p in peers:
         pl.semaphore_signal(barrier, inc=1, device_id=p, device_id_type=MESH)
@@ -112,8 +112,8 @@
     W[core, x, zl, 3:5, 0:76] = kv_in[...]
     FX[x] = jnp.concatenate([fw_in[...], jnp.zeros((64, 52), BF)], axis=1)
     o = ow_in[...]
-    OW[core, x, zh, zl, 0:64] = o[:, :128]
-    OW[core, x, zh, zl, 64:80] = jnp.concatenate(
+    OW[core, x, zl, zh, 0:64] = o[:, :128]
+    OW[core, x, zl, zh, 64:80] = jnp.concatenate(
         [o[16 * g:16 * g + 16, 128:152] for g in range(4)] + [jnp.zeros((16, 32), BF)], axis=1)
     mp[...] = jnp.zeros_like(mp)
     pl.semaphore_wait(barrier, len(peers))
@@ -125,33 +125,78 @@
     def relay(a, to, got):
         return send(a, a, to, got)
 
+    LO, HI = [(0, 80)], [(80, 72)]
+
     class Rows:
         def __init__(self, z):
-            self.z, self.got = z, {}
-
-        def out(self, ch, name):
-            z = self.z
-            self.got[name] = (relay(X.at[y, z, ch], at_y(1), X.at[up(y, -1), z, ch]),
-                              relay(X.at[y, z, ch], at_y(-1), X.at[up(y, 1), z, ch]))
-
-        def on(self):
-            z = self.z
-            self.got["lo"][0]()
-            f = relay(X.at[up(y, -1), z, lo], at_y(1), X.at[up(y, 2), z, lo])
-            self.got["hi"][1]()
-            g = relay(X.at[up(y, 1), z, hi], at_y(-1), X.at[up(y, 2), z, hi])
-            self.rest = [self.got["hi"][0], self.got["lo"][1], f, g]
+            self.z, self.low, self.high, self.rest = z, [], [], []
+
+        def out(self, chunks):
+            for first, size in chunks:
+                ch = pl.ds(first, size)
+                a = X.at[y, self.z, ch]
+                got = (relay(a, at_y(1), X.at[up(y, -1), self.z, ch]), relay(a, at_y(-1), X.at[up(y, 1), self.z, ch]))
+                if first < 80:
+                    self.low.append((got[0], ch))
+                    self.rest.append(got[1])
+                else:
+                    self.high.append((got[1], ch))
+                    self.rest.append(got[0])
+
+        def on(self, which):
+            for wait, ch in which:
+                e = -1 if which is self.low else 1
+                wait()
+                a = X.at[up(y, e), self.z, ch]
+                self.rest.append(relay(a, at_y(-e), X.at[up(y, 2), self.z, ch]))
 
         def done(self):
             all_of(self.rest)
 
+    def along_z(buf, first=None):
+        a = buf(zh)
+        return relay(a, at_zh(1), buf(up(zh, -1))), relay(a, at_zh(-1), buf(up(zh, 1)))
+
+    def on_z(buf, waits):
+        all_of(waits)
+        return relay(buf(up(zh, -1)), at_zh(1), buf(up(zh, 2)))
+
+    def x_out(part):
+        a = part(x)
+        return relay(a, at_x(1), part(up(x, -1))), relay(a, at_x(-1), part(up(x, 1)))
+
+    def x_on(part, waits, n):
+        waits[0]()
+        t, u = pl.ds(0, n[0]), pl.ds(n[0], n[1])
+        f = relay(part(up(x, -1)).at[t], at_x(1), part(up(x, 2)).at[t])
+        waits[1]()
+        g = relay(part(up(x, 1)).at[u], at_x(-1), part(up(x, 2)).at[u])
+        return f, g
+
+    def w_part(d):
+        return lambda i: W.at[core, i, up(zl, d)]
+
+    def across(ref, d):
+        return relay(ref.at[core, :, up(zl, d)], partner, ref.at[1 - core, :, up(zl, d)])
+
     rows = [Rows(zh), Rows(up(zh, -1)), Rows(up(zh, 1)), Rows(up(zh, 2))]
-    ss_z = [relay(SS.at[y, zh], at_zh(d), SS.at[y, up(zh, -d)]) for d in three]
-    rows[0].out(lo, "lo")
-    rows[0].out(hi, "hi")
-    w_z = [relay(W.at[core, x, zl], at_zl(d), W.at[core, x, up(zl, -d)]) for d in three]
-    zp_lo = relay(X.at[y, zh, lo], at_zh(1), X.at[y, up(zh, -1), lo])
-    zm_hi = relay(X.at[y, zh, hi], at_zh(-1), X.at[y, up(zh, 1), hi])
+    ss_z = along_z(lambda z: SS.at[y, z])
+    w_x0 = x_out(w_part(0))
+    rows[0].out(LO + HI)
+    C0, C1, C2, C3 = (0, 48), (48, 32), (80, 48), (128, 24)
+
+    def z_up(c):
+        ch = pl.ds(*c)
+        return relay(X.at[y, zh, ch], at_zh(1), X.at[y, up(zh, -1), ch])
+
+    def z_down(c):
+        ch = pl.ds(*c)
+        return relay(X.at[y, zh, ch], at_zh(-1), X.at[y, up(zh, 1), ch])
+
+    def w_to(d):
+        return relay(W.at[core, x, zl], at_zl(d), W.at[core, x, up(zl, -d)])
+
+    zp_0, zm_2 = z_up(C0), z_down(C2)
 
     c = cond[...]
     act = (c * jax.nn.sigmoid(c)).astype(BF)
@@ -165,41 +210,54 @@
     all_of(mods)
     ms[...] = (mx[0] + mx[1]) + (mx[2] + mx[3])
     mods = [send(ms.at[up(zl, d)], ml.at[zl], at_zl(d), ml.at[up(zl, -d)]) for d in three]
-    zp_hi = relay(X.at[y, zh, hi], at_zh(1), X.at[y, up(zh, -1), hi])
-    zm_lo = relay(X.at[y, zh, lo], at_zh(-1), X.at[y, up(zh, 1), lo])
-    all_of(ss_z)
-    ss_y = [relay(SS.at[y], at_y(d), SS.at[up(y, -d)]) for d in three]
+    zp_1, zm_3 = z_up(C1), z_down(C3)
     ml[zl] = ms[zl]
-
-    def x_out(part):
-        a = part(x)
-        return relay(a, at_x(1), part(up(x, -1))), relay(a, at_x(-1), part(up(x, 1)))
-
-    def x_on(part, waits):
-        waits[0]()
-        t, u = pl.ds(0, 2), pl.ds(2, 2)
-        f = relay(part(up(x, -1)).at[t], at_x(1), part(up(x, 2)).at[t])
-        waits[1]()
-        g = relay(part(up(x, 1)).at[u], at_x(-1), part(up(x, 2)).at[u])
-        return f, g
-
-    def w_part(i):
-        return W.at[core, i]
-
-    def across(d):
-        return relay(W.at[core, up(x, d)], partner, W.at[1 - core, up(x, d)])
-
-    rows[0].on()
-    all_of(w_z)
-    w_x = x_out(w_part)
-    w_a = [across(0)]
-    zp_lo()
-    rows[1].out(lo, "lo")
-    zm_hi()
-    rows[2].out(hi, "hi")
+    w_x0 = x_on(w_part(0), w_x0, (3, 2))
+    ss_f = on_z(lambda z: SS.at[y, z], ss_z)
+    rows[0].on(rows[0].low)
+    rows[0].on(rows[0].high)
     all_of(mods)
     tot[core] = (ml[0] + ml[1]) + (ml[2] + ml[3])
     tw = relay(tot.at[core], partner, tot.at[1 - core])
+    tw()
+    M[y, zh] = tot[0] + tot[1]
+    m_z = along_z(lambda z: M.at[y, z])
+    w_z = [w_to(1), w_to(3)]
+    ss_f()
+    ss_y = [relay(SS.at[y], at_y(d), SS.at[up(y, -d)]) for d in three]
+    all_of(w_x0)
+    w_a = [across(W, 0)]
+    m_f = on_z(lambda z: M.at[y, z], m_z)
+    w_z.append(w_to(2))
+    zp_2, zm_1 = z_up(C2), z_down(C1)
+    w_z[0]()
+    w_x3 = x_out(w_part(-1))
+    w_z[1]()
+    w_x1 = x_out(w_part(1))
+    zp_0()
+    rows[1].out([C0])
+    zm_2()
+    rows[2].out([C2])
+    zp_3, zm_0 = z_up(C3), z_down(C0)
+    m_f()
+    m_y = [relay(M.at[y], at_y(d), M.at[up(y, -d)]) for d in three]
+    w_x3 = x_on(w_part(-1), w_x3, (3, 2))
+    w_x1 = x_on(w_part(1), w_x1, (3, 2))
+    all_of(f_x)
+    FW[core, zl] = FX[y]
+    zp_1()
+    rows[1].out([C1])
+    zm_3()
+    rows[2].out([C3])
+    zpf = []
+    for c in (C0, C1):
+        ch = pl.ds(*c)
+        zpf.append(relay(X.at[y, up(zh, -1), ch], at_zh(1), X.at[y, up(zh, 2), ch]))
+    for c in (C2, C3):
+        ch = pl.ds(*c)
+        zpf.append(relay(X.at[y, up(zh, 1), ch], at_zh(-1), X.at[y, up(zh, 2), ch]))
+    w_z[2]()
+    w_x2 = x_out(w_part(2))
     all_of(ss_y)
     s = jnp.zeros((2, 640), F32)
     for i in range(16):
@@ -207,29 +265,28 @@
     s = s / WIDTH
     mean = s[0:1]
     rs = lax.rsqrt(s[1:2] - mean * mean + EPS_NORM)
-    tw()
-    M[y, zh] = tot[0] + tot[1]
-    m_z = [relay(M.at[y, zh], at_zh(d), M.at[y, up(zh, -d)]) for d in three]
-    zpf = relay(X.at[y, up(zh, -1), lo], at_zh(1), X.at[y, up(zh, 2), lo])
-    zmf = relay(X.at[y, up(zh, 1), hi], at_zh(-1), X.at[y, up(zh, 2), hi])
-    all_of(f_x)
-    FW[core, zl] = FX[y]
-    o_l = [relay(OW.at[core, x, zh, zl], at_zl(d), OW.at[core, x, zh, up(zl, -d)]) for d in three]
+    o_h = along_z(lambda z: OW.at[core, x, zl, z])
+    all_of(w_x3)
+    w_a.append(across(W, -1))
+    all_of(w_x1)
+    w_a.append(across(W, 1))
+    w_x2 = x_on(w_part(2), w_x2, (3, 2))
+    zp_2()
+    rows[1].out([C2])
+    zm_1()
+    rows[2].out([C1])
+    rows[1].on(rows[1].low)
+    rows[2].on(rows[2].high)
+    rows[0].done()
+    zp_3()
+    rows[1].out([C3])
+    zm_0()
+    rows[2].out([C0])
     f_z = [relay(FW.at[core, zl], at_zl(d), FW.at[core, up(zl, -d)]) for d in three]
-    w_xf = x_on(w_part, w_x)
-    w_a += [across(-1), across(1)]
-    zp_hi()
-    rows[1].out(hi, "hi")
-    zm_lo()
-    rows[2].out(lo, "lo")
-    rows[0].done()
-    all_of(w_xf)
-    w_a.append(across(2))
-    rows[1].on()
-    rows[2].on()
+    all_of(w_x2)
+    w_a.append(across(W, 2))
+    o_hf = on_z(lambda z: OW.at[core, x, zl, z], o_h)
     all_of(w_a)
-    all_of(m_z)
-    m_y = [relay(M.at[y], at_y(d), M.at[up(y, -d)]) for d in three]
 
     def join(i, carry):
         xx, ll = lax.rem(i, 4), up(zh, i // 4)
@@ -241,7 +298,10 @@
         return carry
 
     lax.fori_loop(0, 16, join, 0)
-    all_of(m_y)
+    rows[1].on(rows[1].high)
+    rows[2].on(rows[2].low)
+    o_hf()
+    o_l = [relay(OW.at[core, x, zl], at_zl(d), OW.at[core, x, up(zl, -d)]) for d in three]
 
     def ready(k):
         def one(i, carry):
@@ -261,72 +321,66 @@
         lanes = slice(0, 512) if image else slice(512, 640)
         return tdot(W2[n:n + 640, a:b], R[n:n + 640, lanes])
 
+    def o_part(d):
+        return lambda i: OW.at[core, i, up(zl, d)]
+
+    def background():
+        def fan(d):
+            part = o_part(d)
+            return [relay(part(x), at_x(e), part(up(x, -e))) for e in three]
+
+        x0 = fan(0)
+        yield
+        o_l[0]()
+        x3 = fan(-1)
+        o_l[1]()
+        x1 = fan(1)
+        yield
+        o_l[2]()
+        x2 = fan(2)
+        all_of(x0)
+        last = [across(OW, 0)]
+        yield
+        yield
+        all_of(x3)
+        last.append(across(OW, -1))
+        all_of(x1)
+        last.append(across(OW, 1))
+        yield
+        yield
+        all_of(x2)
+        last.append(across(OW, 2))
+        all_of(last)
+        yield
+
+    def add(k):
+        ready(k)
+        PI[...] += dots(k, 0, 384, True)
+        PT[...] += dots(k, 384, 640, False)
+
+    work = background()
+    all_of(m_y)
     ready(0)
     PI[...] = dots(0, 0, 384, True)
     PT[...] = dots(0, 384, 640, False)
-    zpf()
-    rows[3].out(lo, "lo")
-    zmf()
-    rows[3].out(hi, "hi")
-
-    def o_part(d):
-        return lambda i: OW.at[core, i, up(zh, d)]
-
-    def o_across(d):
-        z = up(zh, d)
-        return relay(OW.at[core, :, z], partner, OW.at[1 - core, :, z])
-
-    def background():
-        all_of(o_l)
-        a, t, u = OW.at[core, x], pl.ds(0, 2), pl.ds(2, 2)
-        zp = relay(a.at[zh], at_zh(1), a.at[up(zh, -1)])
-        zm = relay(a.at[zh], at_zh(-1), a.at[up(zh, 1)])
-        x0 = x_out(o_part(0))
-        yield
-        x0 = x_on(o_part(0), x0)
-        yield
-        zp()
-        zpf = relay(a.at[up(zh, -1), t], at_zh(1), a.at[up(zh, 2), t])
-        x3 = x_out(o_part(-1))
-        zm()
-        zmf = relay(a.at[up(zh, 1), u], at_zh(-1), a.at[up(zh, 2), u])
-        x1 = x_out(o_part(1))
-        all_of(x0)
-        last = [o_across(0)]
-        yield
-        x3 = x_on(o_part(-1), x3)
-        x1 = x_on(o_part(1), x1)
-        yield
-        zpf()
-        zmf()
-        x2 = x_out(o_part(2))
-        all_of(x3)
-        last.append(o_across(-1))
-        all_of(x1)
-        last.append(o_across(1))
-        yield
-        x2 = x_on(o_part(2), x2)
-        yield
-        all_of(x2)
-        last.append(o_across(2))
-        yield
-        all_of(last)
-        yield
-
-    work = background()
+    zpf[0]()
+    rows[3].out([C0])
+    zpf[2]()
+    rows[3].out([C2])
+    next(work, None)
+    rows[1].done()
+    add(3)
+    zpf[1]()
+    rows[3].out([C1])
+    zpf[3]()
+    rows[3].out([C3])
+    rows[2].done()
+    add(1)
+    rows[3].on(rows[3].low)
+    rows[3].on(rows[3].high)
     all_of(f_z)
     f_a = [relay(FW.at[core], partner, FW.at[1 - core])]
-    next(work)
-    rows[1].done()
-    ready(3)
-    PI[...] += dots(3, 0, 384, True)
-    PT[...] += dots(3, 384, 640, False)
-    rows[2].done()
-    ready(1)
-    PI[...] += dots(1, 0, 384, True)
-    PT[...] += dots(1, 384, 640, False)
-    rows[3].on()
-    next(work)
+    next(work, None)
     rows[3].done()
     ready(2)
 
@@ -343,15 +397,16 @@
     tkv = PT[...] + dots(2, 384, 640, False)
     KB[0, :512] = two(kv[:128], G[:, 1:2]).T.astype(BF)
     KB[0, 512:] = two(tkv[:128], G[:, 2:3]).T.astype(BF)
-    VB[0, :, :512] = kv[128:].astype(BF)
-    VB[0, :, 512:] = tkv[128:].astype(BF)
+    VB[0, :128, :512] = kv[128:].astype(BF)
+    VB[0, :128, 512:] = tkv[128:].astype(BF)
+    VB[0, 128:] = jnp.ones((16, 640), BF)
     waits = [send(KB.at[0], KB.at[1], partner, KB.at[1]), send(VB.at[0], VB.at[1], partner, VB.at[1])]
     qt = two(PI[0:128] + dots(2, 0, 128, True), G[:, 0:1])
     head = lax.broadcasted_iota(jnp.int32, (128, 512), 0) // 64
-    qz = [jnp.where(head == h, qt, 0.0).astype(BF) for h in range(2)]
+    qz = [jnp.where(head == h, qt, 0.0).astype(BF) * 0.125 for h in range(2)]
     for t in range(4):
         QC[t] = jnp.concatenate([qz[0][:, 128 * t:128 * t + 128], qz[1][:, 128 * t:128 * t + 128]], axis=1)
-    next(work)
+    next(work, None)
     all_of(waits)
 
     length = text_len[me]
@@ -362,19 +417,17 @@
         t = QC[up(zh, d)]
         scores = []
         for j in range(2):
-            sc = jnp.dot(KB[j], t, preferred_element_type=F32) * 0.125
+            sc = jnp.dot(KB[j], t, preferred_element_type=F32)
             scores += [sc[:512], jnp.where(valid[j], sc[512:], -jnp.inf)]
         top = scores[0].max(axis=0, keepdims=True)
         for sc in scores[1:]:
             top = jnp.maximum(top, sc.max(axis=0, keepdims=True))
-        e = [jnp.exp(sc - top) for sc in scores]
-        total = sum(v.sum(axis=0, keepdims=True) for v in e)
-        inv = 1.0 / total
-        p = [(v * inv).astype(BF) for v in e]
+        p = [jnp.exp(sc - top).astype(BF) for sc in scores]
         o = 0.0
         for j in range(2):
             o = o + jnp.dot(VB[j, :, :512], p[2 * j], preferred_element_type=F32)
             o = o + jnp.dot(VB[j, :, 512:], p[2 * j + 1], preferred_element_type=F32)
+        o = o[:128] / o[128:129]
         if d:
             AT[d - 1, 0] = o[:64, :128].astype(BF)
             AT[d - 1, 1] = o[64:, 128:].astype(BF)
@@ -382,7 +435,7 @@
         else:
             A[0, y, zh] = o[:64, :128].astype(BF)
             A[1, y, zh] = o[64:, 128:].astype(BF)
-        next(work)
+        next(work, None)
 
     a_y = []
 
@@ -394,6 +447,8 @@
     for d in (1, 3, 2):
         a_z[d]()
         along_y(up(zh, -d))
+    all_of(f_a)
+    fw = [jnp.concatenate([FW[0, z][:, :76], FW[1, z][:, :76]], axis=1) for z in range(4)]
     for _ in work:
         pass
 
@@ -402,7 +457,7 @@
             t = 0.0
             for h in range(2):
                 a = A[h, yy].reshape(256, 128)
-                w = OW[h, yy, z]
+                w = OW[h, yy, :, z]
                 tail = jnp.concatenate([w[:, 64:80, 24 * g:24 * g + 24] for g in range(4)], axis=1)
                 w = jnp.concatenate([w[:, :64], tail], axis=2).reshape(256, 152)
                 t = t + tdot(a, w)
@@ -424,7 +479,6 @@
     ST[y, 0] = s
     ST[y, 1] = q
     all_of([relay(ST.at[y], at_y(d), ST.at[up(y, -d)]) for d in (1, 3, 2)])
-    all_of(f_a)
     st = ST[0] + ST[1] + (ST[2] + ST[3])
     mean = jnp.sum(st[0], axis=0, keepdims=True) / WIDTH
     square = jnp.sum(st[1], axis=0, keepdims=True) / WIDTH
@@ -433,9 +487,7 @@
     for z in range(4):
         m = M[y, z].T
         head_in = ((U[z].astype(F32) - mean) * rs) * (1.0 + m[:152, 6:7]) + m[:152, 5:6]
-        for h in range(2):
-            vel = vel + jnp.dot(FW[h, z][:, :76], head_in[76 * h:76 * h + 76].astype(BF),
-                                preferred_element_type=F32)
+        vel = vel + jnp.dot(fw[z], head_in.astype(BF), preferred_element_type=F32)
     VP[y] = vel
     all_of([relay(VP.at[y], at_y(d), VP.at[up(y, -d)]) for d in (1, 3, 2)])
     VZ[zh] = (VP[0] + VP[1] + (VP[2] + VP[3])).astype(BF)
@@ -471,7 +523,7 @@
     ((384, 512), F32),
     ((256, 128), F32),
     ((2, 640, 128), BF),
-    ((2, 128, 640), BF),
+    ((2, 144, 640), BF),
     ((4, 128, 256), BF),
     ((3, 2, 64, 128), BF),
     ((2, 4, 4, 64, 128), BF),
@@ -490,7 +542,7 @@
         out_shape=jax.ShapeDtypeStruct((2, 64, 512), F32),
         in_specs=[VMEM] * 10 + [SMEM, SMEM, VMEM],
         out_specs=VMEM,
-        scratch_shapes=[pltpu.VMEM(s, t) for s, t in SCRATCH] + [dma(160), dma(160)],
+        scratch_shapes=[pltpu.VMEM(s, t) for s, t in SCRATCH] + [dma(200), dma(200)],
         compiler_params=pltpu.CompilerParams(collective_id=0, has_side_effects=True, vmem_limit_bytes=60 << 20),
         name="block",
     )(hidden_img.T, hidden_txt.T, qkv_weight.transpose(1, 0, 2), kv_text_weight.transpose(1, 0, 2), out_weight,

time: 122 us -> 120 us (0.984)
  Pallas kernels: 118 us -> 115 us
    pallas_call x1, Pallas kernels: 118 us -> 115 us  [per_device(): pl.pallas_call(block_kernel, out_shape=jax.ShapeDtypeStruct((2, 64, 512),...]
where the time goes in v4:
time: 120 us; the launch traced here: 118 us
  Pallas kernels  115 us (96%)
  local copies, waits for them, and re-layouts  3.08 us (3%)
    pallas_call x1, Pallas kernels, per_device(): pl.pallas_call(block_kernel, out_shape=jax.ShapeDtypeStruct((2, 64, 512),...  115 us

profile of v4, /device:TPU:6, one launch (start us, length us, event | category | flops | bytes accessed | tf_op | source)
XLA Modules:
  0.0 118.5 jit_solution(9278021053207145251)
XLA Ops:
  0.6 1.4 %copy.17 = bf16[76,2,128]{2,0,1:T(8,128)(2,1)} copy(bf16[76,2,128]{2,1,0:T(2,128)(2,1)} %param.21) | data formatting | bytes 77824 | tf_op args[8]
  2.0 114.7 %block.1 = f32[2,64,512]{2,1,0:T(8,128)} custom-call(bf16[152,512]{1,0:T(8,128)(2,1)} %bitcast.20, bf16[152,96]{1,0:T(8,128)(2,1)} %bitcast.23, bf16[3,76,128]{2,1,0:T(8,128)(2,1)} %bitcast.22, bf16[2,76,128]{2,1,0:T(8,128)(2,1)} %bitcast.19, bf16[64,152]{1,0:T(8,128)(2,1)} %ow_in.1, bf16[64,76]{1,0:T(8,128)(2,1)} %bitcast.24, bf16[7,152,76]{2,1,0:T(8,128)(2,1)} %bitcast.18, ...), custom_call_target="tpu_custom_call" | custom-call | tf_op jit(solution)/shard_map/block/pallas_call | solution.py:540
  116.8 1.7 %slice_bitcast_fusion = (f32[512,64]{0,1:T(8,128)}, f32[512,64]{0,1:T(8,128)}) fusion(f32[2,64,512]{2,1,0:T(8,128)} %block.1), kind=kLoop, calls=%fused_computation | loop fusion | bytes 524288 | tf_op jit(solution)/shard_map/transpose | solution.py:550

commit v5 on v4

--- a/solution.py
+++ b/solution.py
@@ -109,7 +109,8 @@
     SS[y, zh] = jnp.concatenate([jnp.sum(v, axis=0, keepdims=True), jnp.sum(v * v, axis=0, keepdims=True)], axis=0)
     W[core, x, zl] = jnp.zeros((5, 80, 128), BF)
     W[core, x, zl, 0:3, 0:76] = qkv_in[...]
-    W[core, x, zl, 3:5, 0:76] = kv_in[...]
+    W[core, x, zl, 3, 0:76] = kv_in[:, 0]
+    W[core, x, zl, 4, 0:76] = kv_in[:, 1]
     FX[x] = jnp.concatenate([fw_in[...], jnp.zeros((64, 52), BF)], axis=1)
     o = ow_in[...]
     OW[core, x, zl, zh, 0:64] = o[:, :128]
@@ -491,7 +492,7 @@
     VP[y] = vel
     all_of([relay(VP.at[y], at_y(d), VP.at[up(y, -d)]) for d in (1, 3, 2)])
     VZ[zh] = (VP[0] + VP[1] + (VP[2] + VP[3])).astype(BF)
-    all_of([relay(VZ.at[zh], at_zh(d), VZ.at[up(zh, -d)]) for d in (1, 3, 2)])
+    all_of([relay(VZ.at[zh], at_zh(d), VZ.at[up(zh, -d)]) for d in (2, 1, 3)])
     now = jnp.full((8, 128), step_index[me], jnp.int32)
     step = (sigma_of(now + 1) - sigma_of(now))[0:1]
     for z in range(4):
@@ -545,7 +546,7 @@
         scratch_shapes=[pltpu.VMEM(s, t) for s, t in SCRATCH] + [dma(200), dma(200)],
         compiler_params=pltpu.CompilerParams(collective_id=0, has_side_effects=True, vmem_limit_bytes=60 << 20),
         name="block",
-    )(hidden_img.T, hidden_txt.T, qkv_weight.transpose(1, 0, 2), kv_text_weight.transpose(1, 0, 2), out_weight,
+    )(hidden_img.T, hidden_txt.T, qkv_weight.transpose(1, 0, 2), kv_text_weight, out_weight,
       final_weight.T, mod_weight.transpose(1, 2, 0), cond, q_gain.reshape(1, 64), k_gain, text_len, step_index, latent.T)
     return out[0].T, out[1].T
 

time: 120 us -> 118 us (0.983)
  local copies, waits for them, and re-layouts: 3.08 us -> 1.69 us
    unnamed x1 -> x0, local copies, waits for them, and re-layouts: 1.4 us -> none
where the time goes in v5:
time: 118 us; the launch traced here: 117 us
  Pallas kernels  115 us (97%)
  local copies, waits for them, and re-layouts  1.69 us (1%)
    pallas_call x1, Pallas kernels, per_device(): pl.pallas_call(block_kernel, out_shape=jax.ShapeDtypeStruct((2, 64, 512),...  115 us

profile of v5, /device:TPU:6, one launch (start us, length us, event | category | flops | bytes accessed | tf_op | source)
XLA Modules:
  0.0 116.9 jit_solution(11476834095058225162)
XLA Ops:
  0.6 114.6 %block.1 = f32[2,64,512]{2,1,0:T(8,128)} custom-call(bf16[152,512]{1,0:T(8,128)(2,1)} %bitcast.16, bf16[152,96]{1,0:T(8,128)(2,1)} %bitcast.19, bf16[3,76,128]{2,1,0:T(8,128)(2,1)} %bitcast.18, bf16[76,2,128]{2,1,0:T(2,128)(2,1)} %kv_in.1, bf16[64,152]{1,0:T(8,128)(2,1)} %ow_in.1, bf16[64,76]{1,0:T(8,128)(2,1)} %bitcast.20, bf16[7,152,76]{2,1,0:T(8,128)(2,1)} %bitcast.15, ...), custom_call_target="tpu_custom_call" | custom-call | tf_op jit(solution)/shard_map/block/pallas_call | solution.py:541
  115.2 1.7 %slice_bitcast_fusion = (f32[512,64]{0,1:T(8,128)}, f32[512,64]{0,1:T(8,128)}) fusion(f32[2,64,512]{2,1,0:T(8,128)} %block.1), kind=kLoop, calls=%fused_computation | loop fusion | bytes 524288 | tf_op jit(solution)/shard_map/transpose | solution.py:551
